TPU v7x, 256 devices: a whole 4x4x8 slice. The times are simulated.
256 devices in a mesh: dp: 32 (over z, y_lo, core), tensor: 8 (over x, y_hi).
Axes of the slice: x: 4, y: 4 (y_hi: 2, y_lo: 2; y = y_hi * 2 + y_lo), z: 8, core: 2. Of those that a mesh axis runs over, the one named last changes fastest.
Arguments:
- projected: bfloat16 [3, 16384, 2560], P(None, 'dp', 'tensor'), may hold values from -40 to 40
- residue_counts: int32 [32], P('dp'), may hold values from 64 to 512, as said below
- migrate_plan: int32 [32], P('dp'), may hold values from 0 to 1, as said below
- out_weight: bfloat16 [2560, 2560], P('tensor', 'dp'), may hold values from -0.125 to 0.125
- out_cotangent: bfloat16 [64, 512, 2560], P('dp', None, 'tensor'), may hold values from -6 to 6
Outputs:
- layer_out: bfloat16 [64, 512, 2560], P('dp', None, 'tensor')
- grad_projected: bfloat16 [3, 16384, 2560], P(None, 'dp', 'tensor')
- grad_weight: float32 [2560, 2560], P('tensor', 'dp')
Inputs may be any that keep to these rules, and one draw needn't show every extreme that they name: `residue_counts`: some tile has all 512 positions real, and some has exactly 64. migrate_plan[o] = 1 exactly where the sum of residue_counts over the 1 tiles of o exceeds that of its partner (o + 16) % 32 by more than 128, else 0; so never both devices of a pair have 1.
All inputs are finite; a program needn't handle non-finite values.
Results may differ from a plain program's by a relative error of at most 0.02.
Values may be sent and summed in bfloat16 or wider, within the bound.
No kernel may reach another device: no remote copies, remote signals or barrier semaphores. Data moves between devices by JAX's collectives and lax.ppermute only.
A program may use at most 128 MiB of HBM per device.

v0:
```python
import functools

import jax
import jax.numpy as jnp
from jax import lax
from jax.experimental import pallas as pl
from jax.experimental.pallas import tpu as pltpu
from jax.sharding import PartitionSpec as P


HEAD_DIM = 64
N_DP = 32
N_TENSOR = 8
X = N_TENSOR // 2
Z = N_DP // 4
BF16 = jnp.bfloat16
F32 = jnp.float32


SMEM = pl.BlockSpec(memory_space=pltpu.SMEM)
VMEM = pl.BlockSpec(memory_space=pltpu.VMEM)

PLACES = ((0, 0), (1, 0), (-1, 0), (2, 0), (0, 1), (1, 1), (-1, 1), (2, 1))

APART = (0, 4, 2, 6, 1, 5, 3, 7)


def dot(a, b, dim_a, dim_b):
    return lax.dot_general(a, b, (((dim_a,), (dim_b,)), ((), ())), preferred_element_type=F32)


def along_dp(value, to):
    return lax.ppermute(value, "dp", [(i, to(i)) for i in range(N_DP)])


def along_tensor(value, dx, dy):
    def to(i):
        return ((i // 2 + dx) % X) * 2 + ((i % 2) ^ dy)

    return lax.ppermute(value, "tensor", [(i, to(i)) for i in range(N_TENSOR)])


def swapped(value):
    pairs = []
    for a in range(Z):
        for j in range(4):
            for b in range(N_TENSOR):
                pairs.append(((4 * a + j) * N_TENSOR + b, (4 * b + j) * N_TENSOR + a))
    return lax.ppermute(value, ("dp", "tensor"), pairs)


def exchanged(value, flip):
    return along_dp(value, lambda i: i ^ flip)


def half_round(value):
    return along_dp(value, lambda i: (i + N_DP // 2) % N_DP)


def tensor_place(dx, dy):
    t = lax.axis_index("tensor")
    return lax.rem(t // 2 + (dx + X), X) * 2 + lax.rem(lax.rem(t, 2) + dy, 2)


def probs_of(q, k, count):
    scores = dot(k, q, 0, 0)
    rows = lax.broadcasted_iota(jnp.int32, scores.shape, 0)
    scores = jnp.where(rows < count, scores, -1000000000.0)
    exponent = jnp.exp(scores - jnp.max(scores, axis=0, keepdims=True))
    return exponent * (1.0 / jnp.sum(exponent, axis=0, keepdims=True))


def forward_kernel(count_ref, qkv_ref, ctx_ref):
    count = count_ref[0]
    live = lax.broadcasted_iota(jnp.int32, (1, ctx_ref.shape[1]), 1) < count
    q = qkv_ref[0] * jnp.asarray(HEAD_DIM ** (-0.5), BF16)
    probs = probs_of(q, qkv_ref[1], count).astype(BF16)
    context = dot(qkv_ref[2], probs, 1, 0)
    ctx_ref[...] = jnp.where(live, context, 0.0).astype(BF16)


def backward_kernel(count_ref, qkv_ref, *refs):
    grad_refs, out_ref = refs[:-1], refs[-1]
    count = count_ref[0]
    grad = functools.reduce(lambda a, b: a + b, [r[...].astype(F32) for r in grad_refs])
    live = lax.broadcasted_iota(jnp.int32, (1, grad.shape[1]), 1) < count
    grad = jnp.where(live, grad, 0.0).astype(BF16)
    scale = jnp.asarray(HEAD_DIM ** (-0.5), BF16)
    q, k, v = qkv_ref[0] * scale, qkv_ref[1], qkv_ref[2]
    probs = probs_of(q, k, count)
    out_ref[2] = dot(grad, probs.astype(BF16), 1, 1).astype(BF16)
    grad_probs = dot(v, grad, 0, 0).astype(BF16).astype(F32)
    inner = jnp.sum(probs * grad_probs, axis=0, keepdims=True)
    grad_scores = (probs * (grad_probs - inner)).astype(BF16)
    out_ref[0] = (dot(k, grad_scores, 1, 0) * HEAD_DIM ** (-0.5)).astype(BF16)
    out_ref[1] = dot(q, grad_scores, 1, 1).astype(BF16)


def heads_call(kernel, count, qkv, grads, out_planes):
    _, columns, length = qkv.shape
    heads = columns // HEAD_DIM
    plane = pl.BlockSpec((HEAD_DIM, length), lambda h: (h, 0))
    planes = pl.BlockSpec((3, HEAD_DIM, length), lambda h: (0, h, 0))
    dots = 6 if out_planes else 2
    return pl.pallas_call(
        kernel,
        grid=(heads,),
        in_specs=[SMEM, planes] + [plane] * len(grads),
        out_specs=planes if out_planes else plane,
        out_shape=jax.ShapeDtypeStruct(
            (3, columns, length) if out_planes else (columns, length), BF16
        ),
        cost_estimate=pl.CostEstimate(
            flops=2 * dots * columns * length * length,
            bytes_accessed=8 * columns * length * 2,
            transcendentals=heads * length * length,
        ),
    )(count, qkv, *grads)


def grad_partial_kernel(cot_ref, w0_ref, wy_ref, wc_ref, wcy_ref, all_ref, *out_refs):
    dp = lax.axis_index("dp")
    z, j = dp // 4, lax.rem(dp, 4)
    yl, c = j // 2, lax.rem(j, 2)
    for ref, flip_y, flip_c in ((w0_ref, 0, 0), (wy_ref, 1, 0), (wc_ref, 0, 1), (wcy_ref, 1, 1)):
        col = lax.rem(yl + flip_y, 2) * 2 + lax.rem(c + flip_c, 2)
        for k, apart in enumerate(APART):
            all_ref[z ^ apart, col] = ref[k]
    for (dx, dy), out_ref in zip(PLACES, out_refs):
        block = all_ref[tensor_place(dx, dy)].reshape(-1, all_ref.shape[3])
        out_ref[...] = dot(block, cot_ref[...], 0, 0).astype(BF16)


def grad_partial(cot, w0, wy, wc, wcy):
    columns, length = cot.shape
    rows = w0.shape[2]
    return pl.pallas_call(
        grad_partial_kernel,
        name="grad_partial",
        in_specs=[VMEM] * 5,
        out_specs=[VMEM] * 9,
        out_shape=[jax.ShapeDtypeStruct((Z, 4, columns // 4, rows), BF16)]
        + [jax.ShapeDtypeStruct((rows, length), BF16)] * 8,
        cost_estimate=pl.CostEstimate(
            flops=2 * 8 * columns * rows * length, bytes_accessed=8_000_000, transcendentals=0
        ),
    )(cot, w0, wy, wc, wcy)


def layer_out_kernel(flag_ref, all_ref, *refs):
    block_refs, (home_ref, guest_ref) = refs[:-2], refs[-2:]
    total = None
    for (dx, dy), block_ref in zip(PLACES, block_refs):
        weight = all_ref[tensor_place(dx, dy)].reshape(-1, all_ref.shape[3])
        term = dot(weight, block_ref[...], 1, 0)
        total = term if total is None else total + term
    sent = flag_ref[0] > 0
    home_ref[...] = jnp.where(sent, 0.0, total).astype(BF16)
    guest_ref[...] = jnp.where(sent, total, 0.0).astype(BF16)


def layer_out_of(flag, weight, blocks):
    rows, length = blocks[0].shape
    columns = 4 * weight.shape[2]
    return pl.pallas_call(
        layer_out_kernel,
        name="layer_out",
        in_specs=[SMEM, VMEM] + [VMEM] * 8,
        out_specs=[VMEM] * 2,
        out_shape=[jax.ShapeDtypeStruct((columns, length), BF16)] * 2,
        cost_estimate=pl.CostEstimate(
            flops=2 * 8 * columns * rows * length, bytes_accessed=6_000_000, transcendentals=0
        ),
    )(flag, weight, *blocks)


def weight_partial_kernel(cot_ref, *refs):
    block_refs, (keep_ref, send_ref, held) = refs[:-3], refs[-3:]
    dp = lax.axis_index("dp")
    z, j = dp // 4, lax.rem(dp, 4)
    yl, c = j // 2, lax.rem(j, 2)
    for (dx, dy), block_ref in zip(PLACES, block_refs):
        held[...] = dot(cot_ref[...], block_ref[...], 1, 1).astype(BF16).reshape(held.shape)
        apart = tensor_place(dx, dy) ^ z
        k = lax.rem(apart, 2) * 4 + lax.rem(apart // 2, 2) * 2 + apart // 4
        for out_ref, flip_c in ((keep_ref, 0), (send_ref, 1)):
            for flip_y in range(2):
                col = lax.rem(yl + flip_y, 2) * 2 + lax.rem(c + flip_c, 2)
                out_ref[flip_y, k] = held[col]


def weight_partial(cot, blocks):
    columns, length = cot.shape
    rows = blocks[0].shape[0]
    out = jax.ShapeDtypeStruct((2, Z, columns // 4, rows), BF16)
    return pl.pallas_call(
        weight_partial_kernel,
        name="weight_partial",
        in_specs=[VMEM] * 9,
        out_specs=[VMEM] * 2,
        out_shape=[out, out],
        scratch_shapes=[pltpu.VMEM((4, columns // 4, rows), BF16)],
        cost_estimate=pl.CostEstimate(
            flops=2 * 8 * columns * rows * length, bytes_accessed=6_000_000, transcendentals=0
        ),
    )(cot, *blocks)


def added(*terms):
    return functools.reduce(lambda a, b: a + b, [t.astype(F32) for t in terms]).astype(BF16)


def step(projected, residue_counts, migrate_plan, out_weight, out_cotangent):
    qkv = jnp.transpose(projected, (0, 2, 1))
    cot_slots = jnp.transpose(out_cotangent, (0, 2, 1))
    sent = migrate_plan[0] > 0

    moved = swapped(out_weight.T)
    guest_cot = half_round(cot_slots[1])

    ctx = heads_call(forward_kernel, residue_counts, qkv, (), False)

    block = {(0, 0): ctx}
    block[0, 1] = along_tensor(ctx, 0, 1)
    block[2, 0] = along_tensor(ctx, 2, 0)
    block[-1, 0] = along_tensor(ctx, 1, 0)
    block[1, 0] = along_tensor(ctx, -1, 0)
    block[-1, 1] = along_tensor(block[0, 1], 1, 0)
    block[1, 1] = along_tensor(block[0, 1], -1, 0)
    block[2, 1] = along_tensor(block[2, 0], 0, 1)
    blocks = [block[place] for place in PLACES]

    stack = moved[None]
    for bit in (4, 2, 1):
        stack = jnp.concatenate([stack, exchanged(stack, 4 * bit)])
    w0 = stack
    wy = exchanged(w0, 2)
    wc = exchanged(w0, 1)
    wcy = exchanged(wy, 1)

    cot = jnp.where(sent, guest_cot, cot_slots[0])
    weight, *parts = grad_partial(cot, w0, wy, wc, wcy)
    part = dict(zip(PLACES, parts))

    from_other = along_tensor(part[2, 1], 0, 1)
    from_left = along_tensor(part[1, 1], 1, 0)
    from_right = along_tensor(part[-1, 1], -1, 0)
    got = [along_tensor(part[1, 0], 1, 0), along_tensor(part[-1, 0], -1, 0)]
    got.append(along_tensor(added(part[2, 0], from_other), 2, 0))
    got.append(along_tensor(added(part[0, 1], from_left, from_right), 0, 1))

    keep, send = weight_partial(cot, blocks)
    both = exchanged(send, 1)
    total = added(keep[0], both[0], exchanged(added(keep[1], both[1]), 2))
    for bit in (1, 2, 4):
        half = total.shape[0] // 2
        total = added(total[:half], exchanged(total[half:], 4 * bit))
    grad_weight = swapped(total[0]).astype(F32).T

    home, guest = layer_out_of(migrate_plan, weight, blocks)
    returned = half_round(guest)
    layer_out = jnp.transpose(jnp.stack([home, returned]), (0, 2, 1))

    grad_qkv = heads_call(backward_kernel, residue_counts, qkv, (part[0, 0], *got), True)
    return layer_out, jnp.transpose(grad_qkv, (0, 2, 1)), grad_weight


def solution(mesh):
    in_specs = (
        P(None, "dp", "tensor"),
        P("dp"),
        P("dp"),
        P("tensor", "dp"),
        P("dp", None, "tensor"),
    )
    out_specs = (P("dp", None, "tensor"), P(None, "dp", "tensor"), P("tensor", "dp"))
    return jax.shard_map(step, mesh=mesh, in_specs=in_specs, out_specs=out_specs, check_vma=False)
```

profile of v0, /device:TPU:36, one launch (start us, length us, event | category | flops | bytes accessed | tf_op | source)
XLA Modules:
  0.0 168.3 jit_solution(17283611822336730576)
XLA Ops:
  1.4 5.7 %shard_map.76.refs_0_ = bf16[320,512]{1,0:T(8,128)(2,1)} custom-call(s32[1]{0:T(128)S(6)} %copy.8.count_ref, bf16[3,320,512]{2,1,0:T(8,128)(2,1)} %bitcast.34), custom_call_target="tpu_custom_call" | custom-call | flops 335544320 | bytes 2621440 | tf_op jit(solution)/shard_map/pallas_call | solution.py:105
  7.1 3.2 %collective-permute-start.11 = (bf16[320,512]{1,0:T(8,128)(2,1)}, bf16[320,512]{1,0:T(8,128)(2,1)S(1)}, u32[]{:S(2)}, u32[]{:S(2)}) collective-permute-start(bf16[320,512]{1,0:T(8,128)(2,1)} %shard_map.76.refs_0_), channel_id=1, source_target_pairs={{0,1},{1,0},{2,3},{3,2},{4,5},{5,4},{6,7},{7,6},{8,9},{9,8},{10,11... | collective-permute-start | bytes 983048 | tf_op jit(solution)/shard_map/ppermute | solution.py:40
  10.3 6.4 %collective-permute-start = (bf16[320,512]{1,0:T(8,128)(2,1)S(1)}, bf16[320,512]{1,0:T(8,128)(2,1)S(1)}, u32[]{:S(2)}, u32[]{:S(2)}) collective-permute-start(bf16[320,512]{1,0:T(8,128)(2,1)S(1)} %slice_bitcast_fusion.1), channel_id=1, source_target_pairs={{0,128},{8,136},{16,144},{24,152},{32,160},{40,168},{48,176},{56,1... | collective-permute-start | bytes 983048 | tf_op jit(solution)/shard_map/ppermute | solution.py:33
  17.2 2.1 %collective-permute-start.8 = (bf16[320,512]{1,0:T(8,128)(2,1)}, bf16[320,512]{1,0:T(8,128)(2,1)S(1)}, u32[]{:S(2)}, u32[]{:S(2)}) collective-permute-start(bf16[320,512]{1,0:T(8,128)(2,1)} %shard_map.76.refs_0_), channel_id=1, source_target_pairs={{0,6},{1,7},{2,0},{3,1},{4,2},{5,3},{6,4},{7,5},{8,14},{9,15},{10,... | collective-permute-start | bytes 983048 | tf_op jit(solution)/shard_map/ppermute | solution.py:40
  19.3 2.8 %collective-permute-start.1 = (bf16[80,320]{1,0:T(8,128)(2,1)S(1)}, bf16[80,320]{1,0:T(8,128)(2,1)S(1)}, u32[]{:S(2)}, u32[]{:S(2)}) collective-permute-start(bf16[80,320]{1,0:T(8,128)(2,1)S(1)} %bitcast.36), channel_id=1, source_target_pairs={{0,0},{1,32},{2,64},{3,96},{4,128},{5,160},{6,192},{7,224},{8,8},{... | collective-permute-start | bytes 153608 | tf_op jit(solution)/shard_map/ppermute | solution.py:49
  22.1 11.7 %collective-permute-done.1 = bf16[80,320]{1,0:T(8,128)(2,1)S(1)} collective-permute-done((bf16[80,320]{1,0:T(8,128)(2,1)S(1)}, bf16[80,320]{1,0:T(8,128)(2,1)S(1)}, u32[]{:S(2)}, u32[]{:S(2)}) %collective-permute-start.1) | collective-permute-done | bytes 51232 | tf_op jit(solution)/shard_map/ppermute | solution.py:49
  35.3 6.7 %collective-permute-done.2 = bf16[1,80,320]{2,1,0:T(8,128)(2,1)S(1)} collective-permute-done((bf16[1,80,320]{2,1,0:T(8,128)(2,1)S(1)}, bf16[1,80,320]{2,1,0:T(8,128)(2,1)S(1)}, u32[]{:S(2)}, u32[]{:S(2)}) %collective-permute-start.2) | collective-permute-done | bytes 51232 | tf_op jit(solution)/shard_map/ppermute | solution.py:33
  42.1 3.6 %collective-permute-start.12 = (bf16[320,512]{1,0:T(8,128)(2,1)S(1)}, bf16[320,512]{1,0:T(8,128)(2,1)S(1)}, u32[]{:S(2)}, u32[]{:S(2)}) collective-permute-start(bf16[320,512]{1,0:T(8,128)(2,1)S(1)} %collective-permute-done.11.refs_4_), channel_id=1, source_target_pairs={{0,6},{1,7},{2,0},{3,1},{4,2},{5,3},{6,4},{7,5},{8,14},{9,15},{10,... | collective-permute-start | bytes 983048 | tf_op jit(solution)/shard_map/ppermute | solution.py:40
  48.1 4.5 %collective-permute-start.3 = (bf16[2,80,320]{2,1,0:T(8,128)(2,1)S(1)}, bf16[2,80,320]{2,1,0:T(8,128)(2,1)S(1)}, u32[]{:S(2)}, u32[]{:S(2)}) collective-permute-start(bf16[2,80,320]{2,1,0:T(8,128)(2,1)S(1)} %pad_maximum_fusion.2), channel_id=1, source_target_pairs={{0,64},{8,72},{16,80},{24,88},{32,96},{40,104},{48,112},{56,120},{... | collective-permute-start | bytes 307208 | tf_op jit(solution)/shard_map/ppermute | solution.py:33
  54.4 4.7 %collective-permute-done.13.refs_6_ = bf16[320,512]{1,0:T(8,128)(2,1)S(1)} collective-permute-done((bf16[320,512]{1,0:T(8,128)(2,1)S(1)}, bf16[320,512]{1,0:T(8,128)(2,1)S(1)}, u32[]{:S(2)}, u32[]{:S(2)}) %collective-permute-start.13) | collective-permute-done | bytes 327712 | tf_op jit(solution)/shard_map/ppermute | solution.py:40
  60.5 5.0 %weight_partial.1 = (bf16[2,8,80,320]{3,2,1,0:T(8,128)(2,1)}, bf16[2,8,80,320]{3,2,1,0:T(8,128)(2,1)}) custom-call(bf16[320,512]{1,0:T(8,128)(2,1)} %fusion.2.cot_ref, bf16[320,512]{1,0:T(8,128)(2,1)} %shard_map.76.refs_0_, bf16[320,512]{1,0:T(8,128)(2,1)} %copy-done.5, bf16[320,512]{1,0:T(8,128)(2,1)} %copy-done.6, bf16[320,512]{1,0:T(8,128)(2,1)} %copy-done.4, ...), custom_call_target="tpu_custom_call" | custom-call | flops 838860800 | bytes 6000000 | tf_op jit(solution)/shard_map/weight_partial/pallas_call | solution.py:196
  65.6 8.3 %collective-permute-done.4 = bf16[4,80,320]{2,1,0:T(8,128)(2,1)S(1)} collective-permute-done((bf16[4,80,320]{2,1,0:T(8,128)(2,1)S(1)}, bf16[4,80,320]{2,1,0:T(8,128)(2,1)S(1)}, u32[]{:S(2)}, u32[]{:S(2)}) %collective-permute-start.4) | collective-permute-done | bytes 204832 | tf_op jit(solution)/shard_map/ppermute | solution.py:33
  75.8 11.2 %collective-permute-done.5.wy_ref = bf16[8,80,320]{2,1,0:T(8,128)(2,1)S(1)} collective-permute-done((bf16[8,80,320]{2,1,0:T(8,128)(2,1)S(1)}, bf16[8,80,320]{2,1,0:T(8,128)(2,1)S(1)}, u32[]{:S(2)}, u32[]{:S(2)}) %collective-permute-start.5) | collective-permute-done | bytes 409632 | tf_op jit(solution)/shard_map/ppermute | solution.py:33
  91.0 4.7 %grad_partial.1 = (bf16[8,4,80,320]{3,2,1,0:T(8,128)(2,1)}, bf16[320,512]{1,0:T(8,128)(2,1)}, bf16[320,512]{1,0:T(8,128)(2,1)}, bf16[320,512]{1,0:T(8,128)(2,1)}...) custom-call(bf16[320,512]{1,0:T(8,128)(2,1)} %fusion.2.cot_ref, ...), custom_call_target="tpu_custom_call" | custom-call | flops 838860800 | bytes 8000000 | tf_op jit(solution)/shard_map/grad_partial/pallas_call | solution.py:137
  95.7 4.2 %collective-permute-start.18 = (bf16[320,512]{1,0:T(8,128)(2,1)}, bf16[320,512]{1,0:T(8,128)(2,1)S(1)}, u32[]{:S(2)}, u32[]{:S(2)}) collective-permute-start(bf16[320,512]{1,0:T(8,128)(2,1)} %get-tuple-element.23), channel_id=1, source_target_pairs={{0,1},{1,0},{2,3},{3,2},{4,5},{5,4},{6,7},{7,6},{8,9},{9,8},{10,11... | collective-permute-start | bytes 983048 | tf_op jit(solution)/shard_map/ppermute | solution.py:40
  99.9 4.7 %layer_out.1 = (bf16[320,512]{1,0:T(8,128)(2,1)}, bf16[320,512]{1,0:T(8,128)(2,1)}) custom-call(s32[1]{0:T(128)S(6)} %copy.9.flag_ref, bf16[8,4,80,320]{3,2,1,0:T(8,128)(2,1)} %get-tuple-element.16.all_ref, bf16[320,512]{1,0:T(8,128)(2,1)} %shard_map.76.refs_0_, bf16[320,512]{1,0:T(8,128)(2,1)} %copy-done.5, bf16[320,512]{1,0:T(8,128)(2,1)} %copy-done.6, ...), custom_call_target="tpu_custom_call" | custom-call | flops 838860800 | bytes 6000000 | tf_op jit(solution)/shard_map/layer_out/pallas_call | solution.py:165
  104.6 5.7 %collective-permute-start.15 = (bf16[320,512]{1,0:T(8,128)(2,1)}, bf16[320,512]{1,0:T(8,128)(2,1)S(1)}, u32[]{:S(2)}, u32[]{:S(2)}) collective-permute-start(bf16[320,512]{1,0:T(8,128)(2,1)} %get-tuple-element.18), channel_id=1, source_target_pairs={{0,128},{8,136},{16,144},{24,152},{32,160},{40,168},{48,176},{56,1... | collective-permute-start | bytes 983048 | tf_op jit(solution)/shard_map/ppermute | solution.py:33
  115.3 12.4 %collective-permute-done.25 = bf16[4,80,320]{2,1,0:T(8,128)(2,1)S(1)} collective-permute-done((bf16[4,80,320]{2,1,0:T(8,128)(2,1)S(1)}, bf16[4,80,320]{2,1,0:T(8,128)(2,1)S(1)}, u32[]{:S(2)}, u32[]{:S(2)}) %collective-permute-start.25) | collective-permute-done | bytes 204832 | tf_op jit(solution)/shard_map/ppermute | solution.py:33
  127.7 3.2 %collective-permute-start.17 = (bf16[320,512]{1,0:T(8,128)(2,1)S(1)}, bf16[320,512]{1,0:T(8,128)(2,1)S(1)}, u32[]{:S(2)}, u32[]{:S(2)}) collective-permute-start(bf16[320,512]{1,0:T(8,128)(2,1)S(1)} %copy-done.15), channel_id=1, source_target_pairs={{0,6},{1,7},{2,0},{3,1},{4,2},{5,3},{6,4},{7,5},{8,14},{9,15},{10,... | collective-permute-start | bytes 983048 | tf_op jit(solution)/shard_map/ppermute | solution.py:40
  131.0 2.4 %collective-permute-start.19 = (bf16[320,512]{1,0:T(8,128)(2,1)S(1)}, bf16[320,512]{1,0:T(8,128)(2,1)S(1)}, u32[]{:S(2)}, u32[]{:S(2)}) collective-permute-start(bf16[320,512]{1,0:T(8,128)(2,1)S(1)} %add_convert_fusion.2), channel_id=1, source_target_pairs={{0,4},{1,5},{2,6},{3,7},{4,0},{5,1},{6,2},{7,3},{8,12},{9,13},{10,... | collective-permute-start | bytes 983048 | tf_op jit(solution)/shard_map/ppermute | solution.py:40
  135.2 4.1 %collective-permute-done.26 = bf16[2,80,320]{2,1,0:T(8,128)(2,1)S(1)} collective-permute-done((bf16[2,80,320]{2,1,0:T(8,128)(2,1)S(1)}, bf16[2,80,320]{2,1,0:T(8,128)(2,1)S(1)}, u32[]{:S(2)}, u32[]{:S(2)}) %collective-permute-start.26) | collective-permute-done | bytes 102432 | tf_op jit(solution)/shard_map/ppermute | solution.py:33
  143.5 5.3 %collective-permute-done.27 = bf16[1,80,320]{2,1,0:T(8,128)(2,1)S(1)} collective-permute-done((bf16[1,80,320]{2,1,0:T(8,128)(2,1)S(1)}, bf16[1,80,320]{2,1,0:T(8,128)(2,1)S(1)}, u32[]{:S(2)}, u32[]{:S(2)}) %collective-permute-start.27) | collective-permute-done | bytes 51232 | tf_op jit(solution)/shard_map/ppermute | solution.py:33
  148.8 8.5 %collective-permute-start.28 = (bf16[80,320]{1,0:T(8,128)(2,1)S(1)}, bf16[80,320]{1,0:T(8,128)(2,1)S(1)}, u32[]{:S(2)}, u32[]{:S(2)}) collective-permute-start(bf16[80,320]{1,0:T(8,128)(2,1)S(1)} %fusion.3), channel_id=1, source_target_pairs={{0,0},{1,32},{2,64},{3,96},{4,128},{5,160},{6,192},{7,224},{8,8},{... | collective-permute-start | bytes 153608 | tf_op jit(solution)/shard_map/ppermute | solution.py:49
  158.8 8.8 %shard_map.77 = bf16[3,320,512]{2,1,0:T(8,128)(2,1)} custom-call(s32[1]{0:T(128)S(6)} %copy.8.count_ref, bf16[3,320,512]{2,1,0:T(8,128)(2,1)} %bitcast.35, bf16[320,512]{1,0:T(8,128)(2,1)} %get-tuple-element.19.refs_0_, bf16[320,512]{1,0:T(8,128)(2,1)} %copy-done.16, bf16[320,512]{1,0:T(8,128)(2,1)} %copy-done.17, bf16[320,512]{1,0:T(8,128)(2,1)} %copy-done.18, ...), custom_call_target="tpu_custom_call" | custom-call | flops 1006632960 | bytes 2621440 | tf_op jit(solution)/shard_map/pallas_call | solution.py:105
  (98 shorter events, 26.0 us)
Async XLA Ops:
  7.1 35.0 %collective-permute-start.11 = (bf16[320,512]{1,0:T(8,128)(2,1)}, bf16[320,512]{1,0:T(8,128)(2,1)S(1)}, u32[]{:S(2)}, u32[]{:S(2)}) collective-permute-start(bf16[320,512]{1,0:T(8,128)(2,1)} %shard_map.76.refs_0_), channel_id=1, source_target_pairs={{0,1},{1,0},{2,3},{3,2},{4,5},{5,4},{6,7},{7,6},{8,9},{9,8},{10,11... | collective-permute-start | bytes 983048 | tf_op jit(solution)/shard_map/ppermute | solution.py:40
  10.3 35.4 %collective-permute-start = (bf16[320,512]{1,0:T(8,128)(2,1)S(1)}, bf16[320,512]{1,0:T(8,128)(2,1)S(1)}, u32[]{:S(2)}, u32[]{:S(2)}) collective-permute-start(bf16[320,512]{1,0:T(8,128)(2,1)S(1)} %slice_bitcast_fusion.1), channel_id=1, source_target_pairs={{0,128},{8,136},{16,144},{24,152},{32,160},{40,168},{48,176},{56,1... | collective-permute-start | bytes 983048 | tf_op jit(solution)/shard_map/ppermute | solution.py:33
  16.7 29.6 %collective-permute-start.10 = (bf16[320,512]{1,0:T(8,128)(2,1)}, bf16[320,512]{1,0:T(8,128)(2,1)S(1)}, u32[]{:S(2)}, u32[]{:S(2)}) collective-permute-start(bf16[320,512]{1,0:T(8,128)(2,1)} %shard_map.76.refs_0_), channel_id=1, source_target_pairs={{0,4},{1,5},{2,6},{3,7},{4,0},{5,1},{6,2},{7,3},{8,12},{9,13},{10,... | collective-permute-start | bytes 983048 | tf_op jit(solution)/shard_map/ppermute | solution.py:40
  17.2 30.9 %collective-permute-start.8 = (bf16[320,512]{1,0:T(8,128)(2,1)}, bf16[320,512]{1,0:T(8,128)(2,1)S(1)}, u32[]{:S(2)}, u32[]{:S(2)}) collective-permute-start(bf16[320,512]{1,0:T(8,128)(2,1)} %shard_map.76.refs_0_), channel_id=1, source_target_pairs={{0,6},{1,7},{2,0},{3,1},{4,2},{5,3},{6,4},{7,5},{8,14},{9,15},{10,... | collective-permute-start | bytes 983048 | tf_op jit(solution)/shard_map/ppermute | solution.py:40
  19.3 14.5 %collective-permute-start.1 = (bf16[80,320]{1,0:T(8,128)(2,1)S(1)}, bf16[80,320]{1,0:T(8,128)(2,1)S(1)}, u32[]{:S(2)}, u32[]{:S(2)}) collective-permute-start(bf16[80,320]{1,0:T(8,128)(2,1)S(1)} %bitcast.36), channel_id=1, source_target_pairs={{0,0},{1,32},{2,64},{3,96},{4,128},{5,160},{6,192},{7,224},{8,8},{... | collective-permute-start | bytes 153608 | tf_op jit(solution)/shard_map/ppermute | solution.py:49
  42.1 12.3 %collective-permute-start.9 = (bf16[320,512]{1,0:T(8,128)(2,1)}, bf16[320,512]{1,0:T(8,128)(2,1)S(1)}, u32[]{:S(2)}, u32[]{:S(2)}) collective-permute-start(bf16[320,512]{1,0:T(8,128)(2,1)} %shard_map.76.refs_0_), channel_id=1, source_target_pairs={{0,2},{1,3},{2,4},{3,5},{4,6},{5,7},{6,0},{7,1},{8,10},{9,11},{10,... | collective-permute-start | bytes 983048 | tf_op jit(solution)/shard_map/ppermute | solution.py:40
  42.1 12.3 %collective-permute-start.12 = (bf16[320,512]{1,0:T(8,128)(2,1)S(1)}, bf16[320,512]{1,0:T(8,128)(2,1)S(1)}, u32[]{:S(2)}, u32[]{:S(2)}) collective-permute-start(bf16[320,512]{1,0:T(8,128)(2,1)S(1)} %collective-permute-done.11.refs_4_), channel_id=1, source_target_pairs={{0,6},{1,7},{2,0},{3,1},{4,2},{5,3},{6,4},{7,5},{8,14},{9,15},{10,... | collective-permute-start | bytes 983048 | tf_op jit(solution)/shard_map/ppermute | solution.py:40
  45.7 13.3 %collective-permute-start.13 = (bf16[320,512]{1,0:T(8,128)(2,1)S(1)}, bf16[320,512]{1,0:T(8,128)(2,1)S(1)}, u32[]{:S(2)}, u32[]{:S(2)}) collective-permute-start(bf16[320,512]{1,0:T(8,128)(2,1)S(1)} %collective-permute-done.11.refs_4_), channel_id=1, source_target_pairs={{0,2},{1,3},{2,4},{3,5},{4,6},{5,7},{6,0},{7,1},{8,10},{9,11},{10,... | collective-permute-start | bytes 983048 | tf_op jit(solution)/shard_map/ppermute | solution.py:40
  46.3 12.8 %collective-permute-start.14 = (bf16[320,512]{1,0:T(8,128)(2,1)S(1)}, bf16[320,512]{1,0:T(8,128)(2,1)S(1)}, u32[]{:S(2)}, u32[]{:S(2)}) collective-permute-start(bf16[320,512]{1,0:T(8,128)(2,1)S(1)} %collective-permute-done.10.refs_3_), channel_id=1, source_target_pairs={{0,1},{1,0},{2,3},{3,2},{4,5},{5,4},{6,7},{7,6},{8,9},{9,8},{10,11... | collective-permute-start | bytes 983048 | tf_op jit(solution)/shard_map/ppermute | solution.py:40
  48.1 17.4 %collective-permute-start.3 = (bf16[2,80,320]{2,1,0:T(8,128)(2,1)S(1)}, bf16[2,80,320]{2,1,0:T(8,128)(2,1)S(1)}, u32[]{:S(2)}, u32[]{:S(2)}) collective-permute-start(bf16[2,80,320]{2,1,0:T(8,128)(2,1)S(1)} %pad_maximum_fusion.2), channel_id=1, source_target_pairs={{0,64},{8,72},{16,80},{24,88},{32,96},{40,104},{48,112},{56,120},{... | collective-permute-start | bytes 307208 | tf_op jit(solution)/shard_map/ppermute | solution.py:33
  65.5 21.5 %collective-permute-start.23 = (bf16[2,8,80,320]{3,2,1,0:T(8,128)(2,1)}, bf16[2,8,80,320]{3,2,1,0:T(8,128)(2,1)S(1)}, u32[]{:S(2)}, u32[]{:S(2)}) collective-permute-start(bf16[2,8,80,320]{3,2,1,0:T(8,128)(2,1)} %get-tuple-element.28), channel_id=1, source_target_pairs={{0,8},{8,0},{16,24},{24,16},{32,40},{40,32},{48,56},{56,48},{64,72... | collective-permute-start | bytes 2457608 | tf_op jit(solution)/shard_map/ppermute | solution.py:33
  74.1 12.9 %collective-permute-start.5 = (bf16[8,80,320]{2,1,0:T(8,128)(2,1)S(1)}, bf16[8,80,320]{2,1,0:T(8,128)(2,1)S(1)}, u32[]{:S(2)}, u32[]{:S(2)}) collective-permute-start(bf16[8,80,320]{2,1,0:T(8,128)(2,1)S(1)} %pad_maximum_fusion.w0_ref), channel_id=1, source_target_pairs={{0,16},{8,24},{16,0},{24,8},{32,48},{40,56},{48,32},{56,40},{64,80... | collective-permute-start | bytes 1228808 | tf_op jit(solution)/shard_map/ppermute | solution.py:33
  75.8 14.4 %collective-permute-start.6 = (bf16[8,80,320]{2,1,0:T(8,128)(2,1)S(1)}, bf16[8,80,320]{2,1,0:T(8,128)(2,1)S(1)}, u32[]{:S(2)}, u32[]{:S(2)}) collective-permute-start(bf16[8,80,320]{2,1,0:T(8,128)(2,1)S(1)} %pad_maximum_fusion.w0_ref), channel_id=1, source_target_pairs={{0,8},{8,0},{16,24},{24,16},{32,40},{40,32},{48,56},{56,48},{64,72... | collective-permute-start | bytes 1228808 | tf_op jit(solution)/shard_map/ppermute | solution.py:33
  88.3 24.0 %collective-permute-start.24 = (bf16[8,80,320]{2,1,0:T(8,128)(2,1)S(1)}, bf16[8,80,320]{2,1,0:T(8,128)(2,1)S(1)}, u32[]{:S(2)}, u32[]{:S(2)}) collective-permute-start(bf16[8,80,320]{2,1,0:T(8,128)(2,1)S(1)} %fusion.1), channel_id=1, source_target_pairs={{0,16},{8,24},{16,0},{24,8},{32,48},{40,56},{48,32},{56,40},{64,80... | collective-permute-start | bytes 1228808 | tf_op jit(solution)/shard_map/ppermute | solution.py:33
  95.7 18.0 %collective-permute-start.18 = (bf16[320,512]{1,0:T(8,128)(2,1)}, bf16[320,512]{1,0:T(8,128)(2,1)S(1)}, u32[]{:S(2)}, u32[]{:S(2)}) collective-permute-start(bf16[320,512]{1,0:T(8,128)(2,1)} %get-tuple-element.23), channel_id=1, source_target_pairs={{0,1},{1,0},{2,3},{3,2},{4,5},{5,4},{6,7},{7,6},{8,9},{9,8},{10,11... | collective-permute-start | bytes 983048 | tf_op jit(solution)/shard_map/ppermute | solution.py:40
  104.6 35.9 %collective-permute-start.15 = (bf16[320,512]{1,0:T(8,128)(2,1)}, bf16[320,512]{1,0:T(8,128)(2,1)S(1)}, u32[]{:S(2)}, u32[]{:S(2)}) collective-permute-start(bf16[320,512]{1,0:T(8,128)(2,1)} %get-tuple-element.18), channel_id=1, source_target_pairs={{0,128},{8,136},{16,144},{24,152},{32,160},{40,168},{48,176},{56,1... | collective-permute-start | bytes 983048 | tf_op jit(solution)/shard_map/ppermute | solution.py:33
  110.3 47.0 %collective-permute-start.16 = (bf16[320,512]{1,0:T(8,128)(2,1)}, bf16[320,512]{1,0:T(8,128)(2,1)S(1)}, u32[]{:S(2)}, u32[]{:S(2)}) collective-permute-start(bf16[320,512]{1,0:T(8,128)(2,1)} %get-tuple-element.20), channel_id=1, source_target_pairs={{0,2},{1,3},{2,4},{3,5},{4,6},{5,7},{6,0},{7,1},{8,10},{9,11},{10,... | collective-permute-start | bytes 983048 | tf_op jit(solution)/shard_map/ppermute | solution.py:40
  110.3 20.7 %collective-permute-start.21 = (bf16[320,512]{1,0:T(8,128)(2,1)}, bf16[320,512]{1,0:T(8,128)(2,1)S(1)}, u32[]{:S(2)}, u32[]{:S(2)}) collective-permute-start(bf16[320,512]{1,0:T(8,128)(2,1)} %get-tuple-element.26), channel_id=1, source_target_pairs={{0,6},{1,7},{2,0},{3,1},{4,2},{5,3},{6,4},{7,5},{8,14},{9,15},{10,... | collective-permute-start | bytes 983048 | tf_op jit(solution)/shard_map/ppermute | solution.py:40
  112.3 21.0 %collective-permute-start.20 = (bf16[320,512]{1,0:T(8,128)(2,1)}, bf16[320,512]{1,0:T(8,128)(2,1)S(1)}, u32[]{:S(2)}, u32[]{:S(2)}) collective-permute-start(bf16[320,512]{1,0:T(8,128)(2,1)} %get-tuple-element.25), channel_id=1, source_target_pairs={{0,2},{1,3},{2,4},{3,5},{4,6},{5,7},{6,0},{7,1},{8,10},{9,11},{10,... | collective-permute-start | bytes 983048 | tf_op jit(solution)/shard_map/ppermute | solution.py:40
  113.7 14.0 %collective-permute-start.25 = (bf16[4,80,320]{2,1,0:T(8,128)(2,1)S(1)}, bf16[4,80,320]{2,1,0:T(8,128)(2,1)S(1)}, u32[]{:S(2)}, u32[]{:S(2)}) collective-permute-start(bf16[4,80,320]{2,1,0:T(8,128)(2,1)S(1)} %slice.53), channel_id=1, source_target_pairs={{0,32},{8,40},{16,48},{24,56},{32,0},{40,8},{48,16},{56,24},{64,96... | collective-permute-start | bytes 614408 | tf_op jit(solution)/shard_map/ppermute | solution.py:33
  127.7 29.7 %collective-permute-start.17 = (bf16[320,512]{1,0:T(8,128)(2,1)S(1)}, bf16[320,512]{1,0:T(8,128)(2,1)S(1)}, u32[]{:S(2)}, u32[]{:S(2)}) collective-permute-start(bf16[320,512]{1,0:T(8,128)(2,1)S(1)} %copy-done.15), channel_id=1, source_target_pairs={{0,6},{1,7},{2,0},{3,1},{4,2},{5,3},{6,4},{7,5},{8,14},{9,15},{10,... | collective-permute-start | bytes 983048 | tf_op jit(solution)/shard_map/ppermute | solution.py:40
  131.0 26.4 %collective-permute-start.19 = (bf16[320,512]{1,0:T(8,128)(2,1)S(1)}, bf16[320,512]{1,0:T(8,128)(2,1)S(1)}, u32[]{:S(2)}, u32[]{:S(2)}) collective-permute-start(bf16[320,512]{1,0:T(8,128)(2,1)S(1)} %add_convert_fusion.2), channel_id=1, source_target_pairs={{0,4},{1,5},{2,6},{3,7},{4,0},{5,1},{6,2},{7,3},{8,12},{9,13},{10,... | collective-permute-start | bytes 983048 | tf_op jit(solution)/shard_map/ppermute | solution.py:40
  139.3 18.1 %collective-permute-start.22 = (bf16[320,512]{1,0:T(8,128)(2,1)S(1)}, bf16[320,512]{1,0:T(8,128)(2,1)S(1)}, u32[]{:S(2)}, u32[]{:S(2)}) collective-permute-start(bf16[320,512]{1,0:T(8,128)(2,1)S(1)} %add_convert_fusion.1), channel_id=1, source_target_pairs={{0,1},{1,0},{2,3},{3,2},{4,5},{5,4},{6,7},{7,6},{8,9},{9,8},{10,11... | collective-permute-start | bytes 983048 | tf_op jit(solution)/shard_map/ppermute | solution.py:40
  148.8 18.8 %collective-permute-start.28 = (bf16[80,320]{1,0:T(8,128)(2,1)S(1)}, bf16[80,320]{1,0:T(8,128)(2,1)S(1)}, u32[]{:S(2)}, u32[]{:S(2)}) collective-permute-start(bf16[80,320]{1,0:T(8,128)(2,1)S(1)} %fusion.3), channel_id=1, source_target_pairs={{0,0},{1,32},{2,64},{3,96},{4,128},{5,160},{6,192},{7,224},{8,8},{... | collective-permute-start | bytes 153608 | tf_op jit(solution)/shard_map/ppermute | solution.py:49
  (26 other events, 238.5 us)
where the time goes:
time: 169 us; the launch traced here: 168 us
  waiting for transfers between devices  65.4 us (39%)
  starting transfers between devices  63.7 us (38%)
  Pallas kernels  28.9 us (17%)
  other arithmetic  4.34 us (3%)
  local copies, waits for them, and re-layouts  3.72 us (2%)
  between operations  2.29 us (1%)
    ppermute x13, waiting for transfers between devices, along_dp(): return lax.ppermute(value, 'dp', [(i, to(i)) for i in range(N_DP)])  48 us
    ppermute x13, starting transfers between devices, along_dp(): return lax.ppermute(value, 'dp', [(i, to(i)) for i in range(N_DP)])  26.5 us
    ppermute x14, starting transfers between devices, along_tensor(): return lax.ppermute(value, 'tensor', [(i, to(i)) for i in range(N_TENSOR)])  25.9 us
    pallas_call x2, Pallas kernels, heads_call(): pl.pallas_call(kernel, grid=(heads,), in_specs=[SMEM, planes] + [plane] *...  14.5 us
    ppermute x2, waiting for transfers between devices, swapped(): return lax.ppermute(value, ('dp', 'tensor'), pairs)  11.7 us
    ppermute x2, starting transfers between devices, swapped(): return lax.ppermute(value, ('dp', 'tensor'), pairs)  11.3 us
    ppermute x14, waiting for transfers between devices, along_tensor(): return lax.ppermute(value, 'tensor', [(i, to(i)) for i in range(N_TENSOR)])  5.63 us
    pallas_call x1, Pallas kernels, weight_partial(): pl.pallas_call(weight_partial_kernel, name='weight_partial', in_specs=[VM...  4.96 us
  transfers between devices with their start and end apart: 29, of which 9 were waited for; matrix products, arithmetic and copies ran while one was open for 2% of the time, Pallas kernels for 14%

commit v1 on v0

--- a/solution.py
+++ b/solution.py
@@ -40,12 +40,21 @@
     return lax.ppermute(value, "tensor", [(i, to(i)) for i in range(N_TENSOR)])
 
 
-def swapped(value):
+def swapped(value, flip):
     pairs = []
     for a in range(Z):
         for j in range(4):
             for b in range(N_TENSOR):
-                pairs.append(((4 * a + j) * N_TENSOR + b, (4 * b + j) * N_TENSOR + a))
+                pairs.append(((4 * a + j) * N_TENSOR + b, (4 * (b ^ flip) + j) * N_TENSOR + a))
+    return lax.ppermute(value, ("dp", "tensor"), pairs)
+
+
+def swapped_back(value, flip):
+    pairs = []
+    for a in range(Z):
+        for j in range(4):
+            for b in range(N_TENSOR):
+                pairs.append(((4 * a + j) * N_TENSOR + b, (4 * b + j) * N_TENSOR + (a ^ flip)))
     return lax.ppermute(value, ("dp", "tensor"), pairs)
 
 
@@ -215,7 +224,7 @@
     cot_slots = jnp.transpose(out_cotangent, (0, 2, 1))
     sent = migrate_plan[0] > 0
 
-    moved = swapped(out_weight.T)
+    moved = [swapped(out_weight.T, flip) for flip in (0, 4)]
     guest_cot = half_round(cot_slots[1])
 
     ctx = heads_call(forward_kernel, residue_counts, qkv, (), False)
@@ -230,8 +239,8 @@
     block[2, 1] = along_tensor(block[2, 0], 0, 1)
     blocks = [block[place] for place in PLACES]
 
-    stack = moved[None]
-    for bit in (4, 2, 1):
+    stack = jnp.stack(moved)
+    for bit in (2, 1):
         stack = jnp.concatenate([stack, exchanged(stack, 4 * bit)])
     w0 = stack
     wy = exchanged(w0, 2)
@@ -252,10 +261,11 @@
     keep, send = weight_partial(cot, blocks)
     both = exchanged(send, 1)
     total = added(keep[0], both[0], exchanged(added(keep[1], both[1]), 2))
-    for bit in (1, 2, 4):
+    for bit in (1, 2):
         half = total.shape[0] // 2
         total = added(total[:half], exchanged(total[half:], 4 * bit))
-    grad_weight = swapped(total[0]).astype(F32).T
+    sums = [swapped_back(total[i], flip) for i, flip in ((0, 0), (1, 4))]
+    grad_weight = (sums[0].astype(F32) + sums[1].astype(F32)).T
 
     home, guest = layer_out_of(migrate_plan, weight, blocks)
     returned = half_round(guest)

time: 169 us -> 161 us (0.953)
  the two profiles are of different devices: /device:TPU:36 before, /device:TPU:20 now
where the time goes in v1:
time: 161 us; the launch traced here: 160 us
  starting transfers between devices  87.3 us (54%)
  waiting for transfers between devices  34.4 us (21%)
  Pallas kernels  28.8 us (18%)
  other arithmetic  4.11 us (3%)
  local copies, waits for them, and re-layouts  3.58 us (2%)
  between operations  2.21 us (1%)
    ppermute x14, starting transfers between devices, along_tensor(): return lax.ppermute(value, 'tensor', [(i, to(i)) for i in range(N_TENSOR)])  38.9 us
    ppermute x2, starting transfers between devices, swapped_back(): return lax.ppermute(value, ('dp', 'tensor'), pairs)  21.6 us
    ppermute x11, waiting for transfers between devices, along_dp(): return lax.ppermute(value, 'dp', [(i, to(i)) for i in range(N_DP)])  19.5 us
    pallas_call x2, Pallas kernels, heads_call(): pl.pallas_call(kernel, grid=(heads,), in_specs=[SMEM, planes] + [plane] *...  14.5 us
    ppermute x2, starting transfers between devices, swapped(): return lax.ppermute(value, ('dp', 'tensor'), pairs)  14.5 us
    ppermute x11, starting transfers between devices, along_dp(): return lax.ppermute(value, 'dp', [(i, to(i)) for i in range(N_DP)])  12.3 us
    ppermute x14, waiting for transfers between devices, along_tensor(): return lax.ppermute(value, 'tensor', [(i, to(i)) for i in range(N_TENSOR)])  12 us
    pallas_call x1, Pallas kernels, weight_partial(): pl.pallas_call(weight_partial_kernel, name='weight_partial', in_specs=[VM...  4.95 us
  transfers between devices with their start and end apart: 29, of which 10 were waited for; matrix products, arithmetic and copies ran while one was open for 3% of the time, Pallas kernels for 18%

profile of v1, /device:TPU:20, one launch (start us, length us, event | category | flops | bytes accessed | tf_op | source)
XLA Modules:
  0.0 160.4 jit_solution(6560467955283229877)
XLA Ops:
  2.4 12.8 %collective-permute-start.1 = (bf16[80,320]{1,0:T(8,128)(2,1)}, bf16[80,320]{1,0:T(8,128)(2,1)S(1)}, u32[]{:S(2)}, u32[]{:S(2)}) collective-permute-start(bf16[80,320]{1,0:T(8,128)(2,1)} %bitcast.42), channel_id=1, source_target_pairs={{0,0},{1,32},{2,64},{3,96},{4,128},{5,160},{6,192},{7,224},{8,8},{... | collective-permute-start | bytes 153608 | tf_op jit(solution)/shard_map/ppermute | solution.py:49
  15.2 3.0 %collective-permute-done.1 = bf16[80,320]{1,0:T(8,128)(2,1)S(1)} collective-permute-done((bf16[80,320]{1,0:T(8,128)(2,1)}, bf16[80,320]{1,0:T(8,128)(2,1)S(1)}, u32[]{:S(2)}, u32[]{:S(2)}) %collective-permute-start.1) | collective-permute-done | bytes 51232 | tf_op jit(solution)/shard_map/ppermute | solution.py:49
  21.2 5.7 %shard_map.76.refs_0_ = bf16[320,512]{1,0:T(8,128)(2,1)} custom-call(s32[1]{0:T(128)S(6)} %copy.8.count_ref, bf16[3,320,512]{2,1,0:T(8,128)(2,1)} %bitcast.39), custom_call_target="tpu_custom_call" | custom-call | flops 335544320 | bytes 2621440 | tf_op jit(solution)/shard_map/pallas_call | solution.py:114
  26.9 17.0 %collective-permute-start.10 = (bf16[320,512]{1,0:T(8,128)(2,1)}, bf16[320,512]{1,0:T(8,128)(2,1)S(1)}, u32[]{:S(2)}, u32[]{:S(2)}) collective-permute-start(bf16[320,512]{1,0:T(8,128)(2,1)} %shard_map.76.refs_0_), channel_id=1, source_target_pairs={{0,4},{1,5},{2,6},{3,7},{4,0},{5,1},{6,2},{7,3},{8,12},{9,13},{10,... | collective-permute-start | bytes 983048 | tf_op jit(solution)/shard_map/ppermute | solution.py:40
  44.9 2.1 %collective-permute-start.9 = (bf16[320,512]{1,0:T(8,128)(2,1)}, bf16[320,512]{1,0:T(8,128)(2,1)S(1)}, u32[]{:S(2)}, u32[]{:S(2)}) collective-permute-start(bf16[320,512]{1,0:T(8,128)(2,1)} %shard_map.76.refs_0_), channel_id=1, source_target_pairs={{0,2},{1,3},{2,4},{3,5},{4,6},{5,7},{6,0},{7,1},{8,10},{9,11},{10,... | collective-permute-start | bytes 983048 | tf_op jit(solution)/shard_map/ppermute | solution.py:40
  47.0 5.8 %collective-permute-done.10.refs_3_ = bf16[320,512]{1,0:T(8,128)(2,1)S(1)} collective-permute-done((bf16[320,512]{1,0:T(8,128)(2,1)}, bf16[320,512]{1,0:T(8,128)(2,1)S(1)}, u32[]{:S(2)}, u32[]{:S(2)}) %collective-permute-start.10) | collective-permute-done | bytes 327712 | tf_op jit(solution)/shard_map/ppermute | solution.py:40
  52.8 3.6 %collective-permute-start.14 = (bf16[320,512]{1,0:T(8,128)(2,1)S(1)}, bf16[320,512]{1,0:T(8,128)(2,1)}, u32[]{:S(2)}, u32[]{:S(2)}) collective-permute-start(bf16[320,512]{1,0:T(8,128)(2,1)S(1)} %collective-permute-done.10.refs_3_), channel_id=1, source_target_pairs={{0,1},{1,0},{2,3},{3,2},{4,5},{5,4},{6,7},{7,6},{8,9},{9,8},{10,11... | collective-permute-start | bytes 983048 | tf_op jit(solution)/shard_map/ppermute | solution.py:40
  57.3 2.3 %collective-permute-start.5 = (bf16[8,80,320]{2,1,0:T(8,128)(2,1)S(1)}, bf16[8,80,320]{2,1,0:T(8,128)(2,1)}, u32[]{:S(2)}, u32[]{:S(2)}) collective-permute-start(bf16[8,80,320]{2,1,0:T(8,128)(2,1)S(1)} %pad_maximum_fusion.w0_ref), channel_id=1, source_target_pairs={{0,16},{8,24},{16,0},{24,8},{32,48},{40,56},{48,32},{56,40},{64,80... | collective-permute-start | bytes 1228808 | tf_op jit(solution)/shard_map/ppermute | solution.py:33
  60.4 5.4 %collective-permute-done.13.refs_6_ = bf16[320,512]{1,0:T(8,128)(2,1)S(1)} collective-permute-done((bf16[320,512]{1,0:T(8,128)(2,1)S(1)}, bf16[320,512]{1,0:T(8,128)(2,1)S(1)}, u32[]{:S(2)}, u32[]{:S(2)}) %collective-permute-start.13) | collective-permute-done | bytes 327712 | tf_op jit(solution)/shard_map/ppermute | solution.py:40
  66.5 5.0 %weight_partial.1 = (bf16[2,8,80,320]{3,2,1,0:T(8,128)(2,1)}, bf16[2,8,80,320]{3,2,1,0:T(8,128)(2,1)}) custom-call(bf16[320,512]{1,0:T(8,128)(2,1)} %fusion.2.cot_ref, bf16[320,512]{1,0:T(8,128)(2,1)} %shard_map.76.refs_0_, bf16[320,512]{1,0:T(8,128)(2,1)} %copy-done.5, bf16[320,512]{1,0:T(8,128)(2,1)} %copy-done.6, bf16[320,512]{1,0:T(8,128)(2,1)} %copy-done.4, ...), custom_call_target="tpu_custom_call" | custom-call | flops 838860800 | bytes 6000000 | tf_op jit(solution)/shard_map/weight_partial/pallas_call | solution.py:205
  72.0 2.3 %collective-permute-done.5.wy_ref = bf16[8,80,320]{2,1,0:T(8,128)(2,1)} collective-permute-done((bf16[8,80,320]{2,1,0:T(8,128)(2,1)S(1)}, bf16[8,80,320]{2,1,0:T(8,128)(2,1)}, u32[]{:S(2)}, u32[]{:S(2)}) %collective-permute-start.5) | collective-permute-done | bytes 409632 | tf_op jit(solution)/shard_map/ppermute | solution.py:33
  77.2 4.6 %grad_partial.1 = (bf16[8,4,80,320]{3,2,1,0:T(8,128)(2,1)}, bf16[320,512]{1,0:T(8,128)(2,1)}, bf16[320,512]{1,0:T(8,128)(2,1)}, bf16[320,512]{1,0:T(8,128)(2,1)}...) custom-call(bf16[320,512]{1,0:T(8,128)(2,1)} %fusion.2.cot_ref, ...), custom_call_target="tpu_custom_call" | custom-call | flops 838860800 | bytes 8000000 | tf_op jit(solution)/shard_map/grad_partial/pallas_call | solution.py:146
  81.8 2.6 %collective-permute-start.18 = (bf16[320,512]{1,0:T(8,128)(2,1)}, bf16[320,512]{1,0:T(8,128)(2,1)}, u32[]{:S(2)}, u32[]{:S(2)}) collective-permute-start(bf16[320,512]{1,0:T(8,128)(2,1)} %get-tuple-element.23), channel_id=1, source_target_pairs={{0,1},{1,0},{2,3},{3,2},{4,5},{5,4},{6,7},{7,6},{8,9},{9,8},{10,11... | collective-permute-start | bytes 983048 | tf_op jit(solution)/shard_map/ppermute | solution.py:40
  84.5 2.3 %collective-permute-start.24 = (bf16[8,80,320]{2,1,0:T(8,128)(2,1)S(1)}, bf16[8,80,320]{2,1,0:T(8,128)(2,1)S(1)}, u32[]{:S(2)}, u32[]{:S(2)}) collective-permute-start(bf16[8,80,320]{2,1,0:T(8,128)(2,1)S(1)} %fusion.1), channel_id=1, source_target_pairs={{0,16},{8,24},{16,0},{24,8},{32,48},{40,56},{48,32},{56,40},{64,80... | collective-permute-start | bytes 1228808 | tf_op jit(solution)/shard_map/ppermute | solution.py:33
  86.8 4.6 %layer_out.1 = (bf16[320,512]{1,0:T(8,128)(2,1)}, bf16[320,512]{1,0:T(8,128)(2,1)}) custom-call(s32[1]{0:T(128)S(6)} %copy.9.flag_ref, bf16[8,4,80,320]{3,2,1,0:T(8,128)(2,1)} %get-tuple-element.16.all_ref, bf16[320,512]{1,0:T(8,128)(2,1)} %shard_map.76.refs_0_, bf16[320,512]{1,0:T(8,128)(2,1)} %copy-done.5, bf16[320,512]{1,0:T(8,128)(2,1)} %copy-done.6, ...), custom_call_target="tpu_custom_call" | custom-call | flops 838860800 | bytes 6000000 | tf_op jit(solution)/shard_map/layer_out/pallas_call | solution.py:174
  92.9 3.2 %collective-permute-start.16 = (bf16[320,512]{1,0:T(8,128)(2,1)}, bf16[320,512]{1,0:T(8,128)(2,1)S(1)}, u32[]{:S(2)}, u32[]{:S(2)}) collective-permute-start(bf16[320,512]{1,0:T(8,128)(2,1)} %get-tuple-element.20), channel_id=1, source_target_pairs={{0,2},{1,3},{2,4},{3,5},{4,6},{5,7},{6,0},{7,1},{8,10},{9,11},{10,... | collective-permute-start | bytes 983048 | tf_op jit(solution)/shard_map/ppermute | solution.py:40
  99.2 5.8 %collective-permute-done.24 = bf16[8,80,320]{2,1,0:T(8,128)(2,1)S(1)} collective-permute-done((bf16[8,80,320]{2,1,0:T(8,128)(2,1)S(1)}, bf16[8,80,320]{2,1,0:T(8,128)(2,1)S(1)}, u32[]{:S(2)}, u32[]{:S(2)}) %collective-permute-start.24) | collective-permute-done | bytes 409632 | tf_op jit(solution)/shard_map/ppermute | solution.py:33
  106.1 4.8 %collective-permute-start.19 = (bf16[320,512]{1,0:T(8,128)(2,1)S(1)}, bf16[320,512]{1,0:T(8,128)(2,1)S(1)}, u32[]{:S(2)}, u32[]{:S(2)}) collective-permute-start(bf16[320,512]{1,0:T(8,128)(2,1)S(1)} %add_convert_fusion.2), channel_id=1, source_target_pairs={{0,4},{1,5},{2,6},{3,7},{4,0},{5,1},{6,2},{7,3},{8,12},{9,13},{10,... | collective-permute-start | bytes 983048 | tf_op jit(solution)/shard_map/ppermute | solution.py:40
  111.0 6.4 %collective-permute-done.25 = bf16[4,80,320]{2,1,0:T(8,128)(2,1)S(1)} collective-permute-done((bf16[4,80,320]{2,1,0:T(8,128)(2,1)S(1)}, bf16[4,80,320]{2,1,0:T(8,128)(2,1)S(1)}, u32[]{:S(2)}, u32[]{:S(2)}) %collective-permute-start.25) | collective-permute-done | bytes 204832 | tf_op jit(solution)/shard_map/ppermute | solution.py:33
  117.5 2.6 %collective-permute-start.22 = (bf16[320,512]{1,0:T(8,128)(2,1)S(1)}, bf16[320,512]{1,0:T(8,128)(2,1)S(1)}, u32[]{:S(2)}, u32[]{:S(2)}) collective-permute-start(bf16[320,512]{1,0:T(8,128)(2,1)S(1)} %add_convert_fusion.1), channel_id=1, source_target_pairs={{0,1},{1,0},{2,3},{3,2},{4,5},{5,4},{6,7},{7,6},{8,9},{9,8},{10,11... | collective-permute-start | bytes 983048 | tf_op jit(solution)/shard_map/ppermute | solution.py:40
  120.2 4.4 %collective-permute-start.26 = (bf16[2,80,320]{2,1,0:T(8,128)(2,1)S(1)}, bf16[2,80,320]{2,1,0:T(8,128)(2,1)S(1)}, u32[]{:S(2)}, u32[]{:S(2)}) collective-permute-start(bf16[2,80,320]{2,1,0:T(8,128)(2,1)S(1)} %slice.55), channel_id=1, source_target_pairs={{0,64},{8,72},{16,80},{24,88},{32,96},{40,104},{48,112},{56,120},{... | collective-permute-start | bytes 307208 | tf_op jit(solution)/shard_map/ppermute | solution.py:33
  125.4 2.8 %collective-permute-done.26 = bf16[2,80,320]{2,1,0:T(8,128)(2,1)S(1)} collective-permute-done((bf16[2,80,320]{2,1,0:T(8,128)(2,1)S(1)}, bf16[2,80,320]{2,1,0:T(8,128)(2,1)S(1)}, u32[]{:S(2)}, u32[]{:S(2)}) %collective-permute-start.26) | collective-permute-done | bytes 102432 | tf_op jit(solution)/shard_map/ppermute | solution.py:33
  130.1 19.8 %collective-permute-start.27 = (bf16[80,320]{1,0:T(8,128)(2,1)S(1)}, bf16[80,320]{1,0:T(8,128)(2,1)S(1)}, u32[]{:S(2)}, u32[]{:S(2)}) collective-permute-start(bf16[80,320]{1,0:T(8,128)(2,1)S(1)} %get-tuple-element.29), channel_id=1, source_target_pairs={{0,0},{1,32},{2,64},{3,96},{4,128},{5,160},{6,192},{7,224},{8,8},{... | collective-permute-start | bytes 153608 | tf_op jit(solution)/shard_map/ppermute | solution.py:58
  150.9 8.8 %shard_map.77 = bf16[3,320,512]{2,1,0:T(8,128)(2,1)} custom-call(s32[1]{0:T(128)S(6)} %copy.8.count_ref, bf16[3,320,512]{2,1,0:T(8,128)(2,1)} %bitcast.40, bf16[320,512]{1,0:T(8,128)(2,1)} %get-tuple-element.19.refs_0_, bf16[320,512]{1,0:T(8,128)(2,1)} %copy-done.14, bf16[320,512]{1,0:T(8,128)(2,1)} %copy-done.15, bf16[320,512]{1,0:T(8,128)(2,1)} %copy-done.16, ...), custom_call_target="tpu_custom_call" | custom-call | flops 1006632960 | bytes 2621440 | tf_op jit(solution)/shard_map/pallas_call | solution.py:114
  (91 shorter events, 20.4 us)
Async XLA Ops:
  0.6 14.5 %collective-permute-start.2 = (bf16[80,320]{1,0:T(8,128)(2,1)}, bf16[80,320]{1,0:T(8,128)(2,1)S(1)}, u32[]{:S(2)}, u32[]{:S(2)}) collective-permute-start(bf16[80,320]{1,0:T(8,128)(2,1)} %bitcast.41), channel_id=1, source_target_pairs={{0,128},{1,160},{2,192},{3,224},{4,0},{5,32},{6,64},{7,96},{8,136}... | collective-permute-start | bytes 153608 | tf_op jit(solution)/shard_map/ppermute | solution.py:49
  2.4 15.8 %collective-permute-start.1 = (bf16[80,320]{1,0:T(8,128)(2,1)}, bf16[80,320]{1,0:T(8,128)(2,1)S(1)}, u32[]{:S(2)}, u32[]{:S(2)}) collective-permute-start(bf16[80,320]{1,0:T(8,128)(2,1)} %bitcast.42), channel_id=1, source_target_pairs={{0,0},{1,32},{2,64},{3,96},{4,128},{5,160},{6,192},{7,224},{8,8},{... | collective-permute-start | bytes 153608 | tf_op jit(solution)/shard_map/ppermute | solution.py:49
  18.2 25.7 %collective-permute-start.3 = (bf16[2,80,320]{2,1,0:T(8,128)(2,1)S(1)}, bf16[2,80,320]{2,1,0:T(8,128)(2,1)S(1)}, u32[]{:S(2)}, u32[]{:S(2)}) collective-permute-start(bf16[2,80,320]{2,1,0:T(8,128)(2,1)S(1)} %pad_maximum_fusion.2), channel_id=1, source_target_pairs={{0,64},{8,72},{16,80},{24,88},{32,96},{40,104},{48,112},{56,120},{... | collective-permute-start | bytes 307208 | tf_op jit(solution)/shard_map/ppermute | solution.py:33
  19.6 25.2 %collective-permute-start = (bf16[320,512]{1,0:T(8,128)(2,1)S(1)}, bf16[320,512]{1,0:T(8,128)(2,1)S(1)}, u32[]{:S(2)}, u32[]{:S(2)}) collective-permute-start(bf16[320,512]{1,0:T(8,128)(2,1)S(1)} %slice_bitcast_fusion.1), channel_id=1, source_target_pairs={{0,128},{8,136},{16,144},{24,152},{32,160},{40,168},{48,176},{56,1... | collective-permute-start | bytes 983048 | tf_op jit(solution)/shard_map/ppermute | solution.py:33
  26.9 20.0 %collective-permute-start.11 = (bf16[320,512]{1,0:T(8,128)(2,1)}, bf16[320,512]{1,0:T(8,128)(2,1)S(1)}, u32[]{:S(2)}, u32[]{:S(2)}) collective-permute-start(bf16[320,512]{1,0:T(8,128)(2,1)} %shard_map.76.refs_0_), channel_id=1, source_target_pairs={{0,1},{1,0},{2,3},{3,2},{4,5},{5,4},{6,7},{7,6},{8,9},{9,8},{10,11... | collective-permute-start | bytes 983048 | tf_op jit(solution)/shard_map/ppermute | solution.py:40
  26.9 25.9 %collective-permute-start.10 = (bf16[320,512]{1,0:T(8,128)(2,1)}, bf16[320,512]{1,0:T(8,128)(2,1)S(1)}, u32[]{:S(2)}, u32[]{:S(2)}) collective-permute-start(bf16[320,512]{1,0:T(8,128)(2,1)} %shard_map.76.refs_0_), channel_id=1, source_target_pairs={{0,4},{1,5},{2,6},{3,7},{4,0},{5,1},{6,2},{7,3},{8,12},{9,13},{10,... | collective-permute-start | bytes 983048 | tf_op jit(solution)/shard_map/ppermute | solution.py:40
  44.1 13.2 %collective-permute-start.8 = (bf16[320,512]{1,0:T(8,128)(2,1)}, bf16[320,512]{1,0:T(8,128)(2,1)S(1)}, u32[]{:S(2)}, u32[]{:S(2)}) collective-permute-start(bf16[320,512]{1,0:T(8,128)(2,1)} %shard_map.76.refs_0_), channel_id=1, source_target_pairs={{0,6},{1,7},{2,0},{3,1},{4,2},{5,3},{6,4},{7,5},{8,14},{9,15},{10,... | collective-permute-start | bytes 983048 | tf_op jit(solution)/shard_map/ppermute | solution.py:40
  44.9 14.8 %collective-permute-start.9 = (bf16[320,512]{1,0:T(8,128)(2,1)}, bf16[320,512]{1,0:T(8,128)(2,1)S(1)}, u32[]{:S(2)}, u32[]{:S(2)}) collective-permute-start(bf16[320,512]{1,0:T(8,128)(2,1)} %shard_map.76.refs_0_), channel_id=1, source_target_pairs={{0,2},{1,3},{2,4},{3,5},{4,6},{5,7},{6,0},{7,1},{8,10},{9,11},{10,... | collective-permute-start | bytes 983048 | tf_op jit(solution)/shard_map/ppermute | solution.py:40
  47.0 13.4 %collective-permute-start.12 = (bf16[320,512]{1,0:T(8,128)(2,1)S(1)}, bf16[320,512]{1,0:T(8,128)(2,1)S(1)}, u32[]{:S(2)}, u32[]{:S(2)}) collective-permute-start(bf16[320,512]{1,0:T(8,128)(2,1)S(1)} %collective-permute-done.11.refs_4_), channel_id=1, source_target_pairs={{0,6},{1,7},{2,0},{3,1},{4,2},{5,3},{6,4},{7,5},{8,14},{9,15},{10,... | collective-permute-start | bytes 983048 | tf_op jit(solution)/shard_map/ppermute | solution.py:40
  52.8 12.9 %collective-permute-start.13 = (bf16[320,512]{1,0:T(8,128)(2,1)S(1)}, bf16[320,512]{1,0:T(8,128)(2,1)S(1)}, u32[]{:S(2)}, u32[]{:S(2)}) collective-permute-start(bf16[320,512]{1,0:T(8,128)(2,1)S(1)} %collective-permute-done.11.refs_4_), channel_id=1, source_target_pairs={{0,2},{1,3},{2,4},{3,5},{4,6},{5,7},{6,0},{7,1},{8,10},{9,11},{10,... | collective-permute-start | bytes 983048 | tf_op jit(solution)/shard_map/ppermute | solution.py:40
  52.8 13.7 %collective-permute-start.14 = (bf16[320,512]{1,0:T(8,128)(2,1)S(1)}, bf16[320,512]{1,0:T(8,128)(2,1)}, u32[]{:S(2)}, u32[]{:S(2)}) collective-permute-start(bf16[320,512]{1,0:T(8,128)(2,1)S(1)} %collective-permute-done.10.refs_3_), channel_id=1, source_target_pairs={{0,1},{1,0},{2,3},{3,2},{4,5},{5,4},{6,7},{7,6},{8,9},{9,8},{10,11... | collective-permute-start | bytes 983048 | tf_op jit(solution)/shard_map/ppermute | solution.py:40
  57.3 16.9 %collective-permute-start.5 = (bf16[8,80,320]{2,1,0:T(8,128)(2,1)S(1)}, bf16[8,80,320]{2,1,0:T(8,128)(2,1)}, u32[]{:S(2)}, u32[]{:S(2)}) collective-permute-start(bf16[8,80,320]{2,1,0:T(8,128)(2,1)S(1)} %pad_maximum_fusion.w0_ref), channel_id=1, source_target_pairs={{0,16},{8,24},{16,0},{24,8},{32,48},{40,56},{48,32},{56,40},{64,80... | collective-permute-start | bytes 1228808 | tf_op jit(solution)/shard_map/ppermute | solution.py:33
  71.5 12.9 %collective-permute-start.23 = (bf16[2,8,80,320]{3,2,1,0:T(8,128)(2,1)}, bf16[2,8,80,320]{3,2,1,0:T(8,128)(2,1)S(1)}, u32[]{:S(2)}, u32[]{:S(2)}) collective-permute-start(bf16[2,8,80,320]{3,2,1,0:T(8,128)(2,1)} %get-tuple-element.28), channel_id=1, source_target_pairs={{0,8},{8,0},{16,24},{24,16},{32,40},{40,32},{48,56},{56,48},{64,72... | collective-permute-start | bytes 2457608 | tf_op jit(solution)/shard_map/ppermute | solution.py:33
  81.8 14.4 %collective-permute-start.18 = (bf16[320,512]{1,0:T(8,128)(2,1)}, bf16[320,512]{1,0:T(8,128)(2,1)}, u32[]{:S(2)}, u32[]{:S(2)}) collective-permute-start(bf16[320,512]{1,0:T(8,128)(2,1)} %get-tuple-element.23), channel_id=1, source_target_pairs={{0,1},{1,0},{2,3},{3,2},{4,5},{5,4},{6,7},{7,6},{8,9},{9,8},{10,11... | collective-permute-start | bytes 983048 | tf_op jit(solution)/shard_map/ppermute | solution.py:40
  84.5 20.5 %collective-permute-start.24 = (bf16[8,80,320]{2,1,0:T(8,128)(2,1)S(1)}, bf16[8,80,320]{2,1,0:T(8,128)(2,1)S(1)}, u32[]{:S(2)}, u32[]{:S(2)}) collective-permute-start(bf16[8,80,320]{2,1,0:T(8,128)(2,1)S(1)} %fusion.1), channel_id=1, source_target_pairs={{0,16},{8,24},{16,0},{24,8},{32,48},{40,56},{48,32},{56,40},{64,80... | collective-permute-start | bytes 1228808 | tf_op jit(solution)/shard_map/ppermute | solution.py:33
  91.5 28.7 %collective-permute-start.15 = (bf16[320,512]{1,0:T(8,128)(2,1)}, bf16[320,512]{1,0:T(8,128)(2,1)S(1)}, u32[]{:S(2)}, u32[]{:S(2)}) collective-permute-start(bf16[320,512]{1,0:T(8,128)(2,1)} %get-tuple-element.18), channel_id=1, source_target_pairs={{0,128},{8,136},{16,144},{24,152},{32,160},{40,168},{48,176},{56,1... | collective-permute-start | bytes 983048 | tf_op jit(solution)/shard_map/ppermute | solution.py:33
  92.9 37.2 %collective-permute-start.16 = (bf16[320,512]{1,0:T(8,128)(2,1)}, bf16[320,512]{1,0:T(8,128)(2,1)S(1)}, u32[]{:S(2)}, u32[]{:S(2)}) collective-permute-start(bf16[320,512]{1,0:T(8,128)(2,1)} %get-tuple-element.20), channel_id=1, source_target_pairs={{0,2},{1,3},{2,4},{3,5},{4,6},{5,7},{6,0},{7,1},{8,10},{9,11},{10,... | collective-permute-start | bytes 983048 | tf_op jit(solution)/shard_map/ppermute | solution.py:40
  96.2 9.9 %collective-permute-start.21 = (bf16[320,512]{1,0:T(8,128)(2,1)}, bf16[320,512]{1,0:T(8,128)(2,1)S(1)}, u32[]{:S(2)}, u32[]{:S(2)}) collective-permute-start(bf16[320,512]{1,0:T(8,128)(2,1)} %get-tuple-element.26), channel_id=1, source_target_pairs={{0,6},{1,7},{2,0},{3,1},{4,2},{5,3},{6,4},{7,5},{8,14},{9,15},{10,... | collective-permute-start | bytes 983048 | tf_op jit(solution)/shard_map/ppermute | solution.py:40
  96.2 14.7 %collective-permute-start.20 = (bf16[320,512]{1,0:T(8,128)(2,1)}, bf16[320,512]{1,0:T(8,128)(2,1)S(1)}, u32[]{:S(2)}, u32[]{:S(2)}) collective-permute-start(bf16[320,512]{1,0:T(8,128)(2,1)} %get-tuple-element.25), channel_id=1, source_target_pairs={{0,2},{1,3},{2,4},{3,5},{4,6},{5,7},{6,0},{7,1},{8,10},{9,11},{10,... | collective-permute-start | bytes 983048 | tf_op jit(solution)/shard_map/ppermute | solution.py:40
  105.1 44.8 %collective-permute-start.17 = (bf16[320,512]{1,0:T(8,128)(2,1)}, bf16[320,512]{1,0:T(8,128)(2,1)S(1)}, u32[]{:S(2)}, u32[]{:S(2)}) collective-permute-start(bf16[320,512]{1,0:T(8,128)(2,1)} %get-tuple-element.21), channel_id=1, source_target_pairs={{0,6},{1,7},{2,0},{3,1},{4,2},{5,3},{6,4},{7,5},{8,14},{9,15},{10,... | collective-permute-start | bytes 983048 | tf_op jit(solution)/shard_map/ppermute | solution.py:40
  106.1 43.8 %collective-permute-start.19 = (bf16[320,512]{1,0:T(8,128)(2,1)S(1)}, bf16[320,512]{1,0:T(8,128)(2,1)S(1)}, u32[]{:S(2)}, u32[]{:S(2)}) collective-permute-start(bf16[320,512]{1,0:T(8,128)(2,1)S(1)} %add_convert_fusion.2), channel_id=1, source_target_pairs={{0,4},{1,5},{2,6},{3,7},{4,0},{5,1},{6,2},{7,3},{8,12},{9,13},{10,... | collective-permute-start | bytes 983048 | tf_op jit(solution)/shard_map/ppermute | solution.py:40
  117.5 32.5 %collective-permute-start.22 = (bf16[320,512]{1,0:T(8,128)(2,1)S(1)}, bf16[320,512]{1,0:T(8,128)(2,1)S(1)}, u32[]{:S(2)}, u32[]{:S(2)}) collective-permute-start(bf16[320,512]{1,0:T(8,128)(2,1)S(1)} %add_convert_fusion.1), channel_id=1, source_target_pairs={{0,1},{1,0},{2,3},{3,2},{4,5},{5,4},{6,7},{7,6},{8,9},{9,8},{10,11... | collective-permute-start | bytes 983048 | tf_op jit(solution)/shard_map/ppermute | solution.py:40
  128.3 31.5 %collective-permute-start.28 = (bf16[80,320]{1,0:T(8,128)(2,1)S(1)}, bf16[80,320]{1,0:T(8,128)(2,1)S(1)}, u32[]{:S(2)}, u32[]{:S(2)}) collective-permute-start(bf16[80,320]{1,0:T(8,128)(2,1)S(1)} %get-tuple-element.30), channel_id=1, source_target_pairs={{0,4},{1,36},{2,68},{3,100},{4,132},{5,164},{6,196},{7,228},{8,12}... | collective-permute-start | bytes 153608 | tf_op jit(solution)/shard_map/ppermute | solution.py:58
  130.1 29.6 %collective-permute-start.27 = (bf16[80,320]{1,0:T(8,128)(2,1)S(1)}, bf16[80,320]{1,0:T(8,128)(2,1)S(1)}, u32[]{:S(2)}, u32[]{:S(2)}) collective-permute-start(bf16[80,320]{1,0:T(8,128)(2,1)S(1)} %get-tuple-element.29), channel_id=1, source_target_pairs={{0,0},{1,32},{2,64},{3,96},{4,128},{5,160},{6,192},{7,224},{8,8},{... | collective-permute-start | bytes 153608 | tf_op jit(solution)/shard_map/ppermute | solution.py:58
  (23 other events, 247.7 us)

commit v2 on v0

--- a/solution.py
+++ b/solution.py
@@ -22,7 +22,7 @@
 
 PLACES = ((0, 0), (1, 0), (-1, 0), (2, 0), (0, 1), (1, 1), (-1, 1), (2, 1))
 
-APART = (0, 4, 2, 6, 1, 5, 3, 7)
+STEPS = (4, 3, 5, 2, 6, 1, 7, 0)
 
 
 def dot(a, b, dim_a, dim_b):
@@ -40,12 +40,18 @@
     return lax.ppermute(value, "tensor", [(i, to(i)) for i in range(N_TENSOR)])
 
 
-def swapped(value):
+def swap_pairs():
     pairs = []
-    for a in range(Z):
+    for t in range(N_TENSOR):
         for j in range(4):
-            for b in range(N_TENSOR):
-                pairs.append(((4 * a + j) * N_TENSOR + b, (4 * b + j) * N_TENSOR + a))
+            for (dx, dy), steps in zip(PLACES, STEPS):
+                rows = ((t // 2 + dx) % X) * 2 + ((t % 2) ^ dy)
+                home = (4 * t + j) * N_TENSOR + rows
+                pairs.append((home, (4 * ((t + steps) % Z) + j) * N_TENSOR + t))
+    return pairs
+
+
+def swapped(value, pairs):
     return lax.ppermute(value, ("dp", "tensor"), pairs)
 
 
@@ -57,9 +63,15 @@
     return along_dp(value, lambda i: (i + N_DP // 2) % N_DP)
 
 
-def tensor_place(dx, dy):
-    t = lax.axis_index("tensor")
-    return lax.rem(t // 2 + (dx + X), X) * 2 + lax.rem(lax.rem(t, 2) + dy, 2)
+def stack_index(steps):
+    z = lax.axis_index("dp") // 4
+    apart = lax.rem(lax.axis_index("tensor") + steps, Z) ^ z
+    return lax.rem(apart, 2) * 4 + lax.rem(apart // 2, 2) * 2 + apart // 4
+
+
+def column_of(flip_y, flip_c):
+    j = lax.rem(lax.axis_index("dp"), 4)
+    return lax.rem(j // 2 + flip_y, 2) * 2 + lax.rem(j + flip_c, 2)
 
 
 def probs_of(q, k, count):
@@ -110,6 +122,7 @@
         out_shape=jax.ShapeDtypeStruct(
             (3, columns, length) if out_planes else (columns, length), BF16
         ),
+        compiler_params=pltpu.CompilerParams(vmem_limit_bytes=16 << 20),
         cost_estimate=pl.CostEstimate(
             flops=2 * dots * columns * length * length,
             bytes_accessed=8 * columns * length * 2,
@@ -119,15 +132,13 @@
 
 
 def grad_partial_kernel(cot_ref, w0_ref, wy_ref, wc_ref, wcy_ref, all_ref, *out_refs):
-    dp = lax.axis_index("dp")
-    z, j = dp // 4, lax.rem(dp, 4)
-    yl, c = j // 2, lax.rem(j, 2)
-    for ref, flip_y, flip_c in ((w0_ref, 0, 0), (wy_ref, 1, 0), (wc_ref, 0, 1), (wcy_ref, 1, 1)):
-        col = lax.rem(yl + flip_y, 2) * 2 + lax.rem(c + flip_c, 2)
-        for k, apart in enumerate(APART):
-            all_ref[z ^ apart, col] = ref[k]
-    for (dx, dy), out_ref in zip(PLACES, out_refs):
-        block = all_ref[tensor_place(dx, dy)].reshape(-1, all_ref.shape[3])
+    for place, (steps, out_ref) in enumerate(zip(STEPS, out_refs)):
+        k = stack_index(steps)
+        all_ref[place, column_of(0, 0)] = w0_ref[k]
+        all_ref[place, column_of(1, 0)] = wy_ref[k]
+        all_ref[place, column_of(0, 1)] = wc_ref[k]
+        all_ref[place, column_of(1, 1)] = wcy_ref[k]
+        block = all_ref[place].reshape(-1, all_ref.shape[3])
         out_ref[...] = dot(block, cot_ref[...], 0, 0).astype(BF16)
 
 
@@ -141,6 +152,7 @@
         out_specs=[VMEM] * 9,
         out_shape=[jax.ShapeDtypeStruct((Z, 4, columns // 4, rows), BF16)]
         + [jax.ShapeDtypeStruct((rows, length), BF16)] * 8,
+        compiler_params=pltpu.CompilerParams(vmem_limit_bytes=16 << 20),
         cost_estimate=pl.CostEstimate(
             flops=2 * 8 * columns * rows * length, bytes_accessed=8_000_000, transcendentals=0
         ),
@@ -150,8 +162,8 @@
 def layer_out_kernel(flag_ref, all_ref, *refs):
     block_refs, (home_ref, guest_ref) = refs[:-2], refs[-2:]
     total = None
-    for (dx, dy), block_ref in zip(PLACES, block_refs):
-        weight = all_ref[tensor_place(dx, dy)].reshape(-1, all_ref.shape[3])
+    for place, block_ref in enumerate(block_refs):
+        weight = all_ref[place].reshape(-1, all_ref.shape[3])
         term = dot(weight, block_ref[...], 1, 0)
         total = term if total is None else total + term
     sent = flag_ref[0] > 0
@@ -168,6 +180,7 @@
         in_specs=[SMEM, VMEM] + [VMEM] * 8,
         out_specs=[VMEM] * 2,
         out_shape=[jax.ShapeDtypeStruct((columns, length), BF16)] * 2,
+        compiler_params=pltpu.CompilerParams(vmem_limit_bytes=16 << 20),
         cost_estimate=pl.CostEstimate(
             flops=2 * 8 * columns * rows * length, bytes_accessed=6_000_000, transcendentals=0
         ),
@@ -176,17 +189,12 @@
 
 def weight_partial_kernel(cot_ref, *refs):
     block_refs, (keep_ref, send_ref, held) = refs[:-3], refs[-3:]
-    dp = lax.axis_index("dp")
-    z, j = dp // 4, lax.rem(dp, 4)
-    yl, c = j // 2, lax.rem(j, 2)
-    for (dx, dy), block_ref in zip(PLACES, block_refs):
+    for steps, block_ref in zip(STEPS, block_refs):
         held[...] = dot(cot_ref[...], block_ref[...], 1, 1).astype(BF16).reshape(held.shape)
-        apart = tensor_place(dx, dy) ^ z
-        k = lax.rem(apart, 2) * 4 + lax.rem(apart // 2, 2) * 2 + apart // 4
-        for out_ref, flip_c in ((keep_ref, 0), (send_ref, 1)):
-            for flip_y in range(2):
-                col = lax.rem(yl + flip_y, 2) * 2 + lax.rem(c + flip_c, 2)
-                out_ref[flip_y, k] = held[col]
+        k = stack_index(steps)
+        for flip_y in range(2):
+            keep_ref[flip_y, k] = held[column_of(flip_y, 0)]
+            send_ref[flip_y, k] = held[column_of(flip_y, 1)]
 
 
 def weight_partial(cot, blocks):
@@ -200,6 +208,7 @@
         out_specs=[VMEM] * 2,
         out_shape=[out, out],
         scratch_shapes=[pltpu.VMEM((4, columns // 4, rows), BF16)],
+        compiler_params=pltpu.CompilerParams(vmem_limit_bytes=16 << 20),
         cost_estimate=pl.CostEstimate(
             flops=2 * 8 * columns * rows * length, bytes_accessed=6_000_000, transcendentals=0
         ),
@@ -215,7 +224,8 @@
     cot_slots = jnp.transpose(out_cotangent, (0, 2, 1))
     sent = migrate_plan[0] > 0
 
-    moved = swapped(out_weight.T)
+    pairs = swap_pairs()
+    moved = swapped(out_weight.T, pairs)
     guest_cot = half_round(cot_slots[1])
 
     ctx = heads_call(forward_kernel, residue_counts, qkv, (), False)
@@ -255,7 +265,8 @@
     for bit in (1, 2, 4):
         half = total.shape[0] // 2
         total = added(total[:half], exchanged(total[half:], 4 * bit))
-    grad_weight = swapped(total[0]).astype(F32).T
+    home_pairs = [(there, here) for here, there in pairs]
+    grad_weight = swapped(total[0], home_pairs).astype(F32).T
 
     home, guest = layer_out_of(migrate_plan, weight, blocks)
     returned = half_round(guest)

time: 169 us -> 149 us (0.88)
  the two profiles are of different devices: /device:TPU:36 before, /device:TPU:1 now
where the time goes in v2:
time: 149 us; the launch traced here: 146 us
  starting transfers between devices  64.6 us (43%)
  waiting for transfers between devices  59.2 us (40%)
  Pallas kernels  16.5 us (11%)
  other arithmetic  2.4 us (2%)
  between operations  2.14 us (1%)
    ppermute x13, waiting for transfers between devices, along_dp(): return lax.ppermute(value, 'dp', [(i, to(i)) for i in range(N_DP)])  39.2 us
    ppermute x14, starting transfers between devices, along_tensor(): return lax.ppermute(value, 'tensor', [(i, to(i)) for i in range(N_TENSOR)])  34.2 us
    ppermute x13, starting transfers between devices, along_dp(): return lax.ppermute(value, 'dp', [(i, to(i)) for i in range(N_DP)])  30.2 us
    ppermute x14, waiting for transfers between devices, along_tensor(): return lax.ppermute(value, 'tensor', [(i, to(i)) for i in range(N_TENSOR)])  12.4 us
    pallas_call x2, Pallas kernels, heads_call(): pl.pallas_call(kernel, grid=(heads,), in_specs=[SMEM, planes] + [plane] *...  11.6 us
    ppermute x2, waiting for transfers between devices, swapped(): return lax.ppermute(value, ('dp', 'tensor'), pairs)  7.54 us
  transfers between devices with their start and end apart: 29, of which 11 were waited for; matrix products, arithmetic and copies ran while one was open for 1% of the time, Pallas kernels for 9%

profile of v2, /device:TPU:1, one launch (start us, length us, event | category | flops | bytes accessed | tf_op | source)
XLA Modules:
  0.0 146.2 jit_solution(9062747760576420712)
XLA Ops:
  2.5 3.8 %shard_map.76.refs_0_ = bf16[320,512]{1,0:T(8,128)(2,1)S(1)} custom-call(s32[1]{0:T(128)S(6)} %copy.8.count_ref, bf16[3,320,512]{2,1,0:T(8,128)(2,1)S(1)} %bitcast.27), custom_call_target="tpu_custom_call" | custom-call | flops 335544320 | bytes 2621440 | tf_op jit(solution)/shard_map/pallas_call | solution.py:117
  6.3 3.8 %collective-permute-start.11 = (bf16[320,512]{1,0:T(8,128)(2,1)S(1)}, bf16[320,512]{1,0:T(8,128)(2,1)S(1)}, u32[]{:S(2)}, u32[]{:S(2)}) collective-permute-start(bf16[320,512]{1,0:T(8,128)(2,1)S(1)} %shard_map.76.refs_0_), channel_id=1, source_target_pairs={{0,1},{1,0},{2,3},{3,2},{4,5},{5,4},{6,7},{7,6},{8,9},{9,8},{10,11... | collective-permute-start | bytes 983048 | tf_op jit(solution)/shard_map/ppermute | solution.py:40
  10.2 7.0 %collective-permute-start = (bf16[320,512]{1,0:T(8,128)(2,1)S(1)}, bf16[320,512]{1,0:T(8,128)(2,1)S(1)}, u32[]{:S(2)}, u32[]{:S(2)}) collective-permute-start(bf16[320,512]{1,0:T(8,128)(2,1)S(1)} %slice_bitcast_fusion.1), channel_id=1, source_target_pairs={{0,128},{8,136},{16,144},{24,152},{32,160},{40,168},{48,176},{56,1... | collective-permute-start | bytes 983048 | tf_op jit(solution)/shard_map/ppermute | solution.py:33
  17.2 2.7 %collective-permute-start.10 = (bf16[320,512]{1,0:T(8,128)(2,1)S(1)}, bf16[320,512]{1,0:T(8,128)(2,1)S(1)}, u32[]{:S(2)}, u32[]{:S(2)}) collective-permute-start(bf16[320,512]{1,0:T(8,128)(2,1)S(1)} %shard_map.76.refs_0_), channel_id=1, source_target_pairs={{0,4},{1,5},{2,6},{3,7},{4,0},{5,1},{6,2},{7,3},{8,12},{9,13},{10,... | collective-permute-start | bytes 983048 | tf_op jit(solution)/shard_map/ppermute | solution.py:40
  20.9 7.5 %collective-permute-done.1 = bf16[80,320]{1,0:T(8,128)(2,1)S(1)} collective-permute-done((bf16[80,320]{1,0:T(8,128)(2,1)S(1)}, bf16[80,320]{1,0:T(8,128)(2,1)S(1)}, u32[]{:S(2)}, u32[]{:S(2)}) %collective-permute-start.1) | collective-permute-done | bytes 51232 | tf_op jit(solution)/shard_map/ppermute | solution.py:55
  28.4 3.9 %collective-permute-start.2 = (bf16[1,80,320]{2,1,0:T(8,128)(2,1)S(1)}, bf16[1,80,320]{2,1,0:T(8,128)(2,1)S(1)}, u32[]{:S(2)}, u32[]{:S(2)}) collective-permute-start(bf16[1,80,320]{2,1,0:T(8,128)(2,1)S(1)} %bitcast.31), channel_id=1, source_target_pairs={{0,128},{8,136},{16,144},{24,152},{32,160},{40,168},{48,176},{56,1... | collective-permute-start | bytes 153608 | tf_op jit(solution)/shard_map/ppermute | solution.py:33
  33.0 4.0 %collective-permute-done.2 = bf16[1,80,320]{2,1,0:T(8,128)(2,1)S(1)} collective-permute-done((bf16[1,80,320]{2,1,0:T(8,128)(2,1)S(1)}, bf16[1,80,320]{2,1,0:T(8,128)(2,1)S(1)}, u32[]{:S(2)}, u32[]{:S(2)}) %collective-permute-start.2) | collective-permute-done | bytes 51232 | tf_op jit(solution)/shard_map/ppermute | solution.py:33
  37.0 5.3 %collective-permute-start.9 = (bf16[320,512]{1,0:T(8,128)(2,1)S(1)}, bf16[320,512]{1,0:T(8,128)(2,1)S(1)}, u32[]{:S(2)}, u32[]{:S(2)}) collective-permute-start(bf16[320,512]{1,0:T(8,128)(2,1)S(1)} %shard_map.76.refs_0_), channel_id=1, source_target_pairs={{0,2},{1,3},{2,4},{3,5},{4,6},{5,7},{6,0},{7,1},{8,10},{9,11},{10,... | collective-permute-start | bytes 983048 | tf_op jit(solution)/shard_map/ppermute | solution.py:40
  43.8 6.2 %collective-permute-start.14 = (bf16[320,512]{1,0:T(8,128)(2,1)S(1)}, bf16[320,512]{1,0:T(8,128)(2,1)S(1)}, u32[]{:S(2)}, u32[]{:S(2)}) collective-permute-start(bf16[320,512]{1,0:T(8,128)(2,1)S(1)} %collective-permute-done.10.refs_3_), channel_id=1, source_target_pairs={{0,1},{1,0},{2,3},{3,2},{4,5},{5,4},{6,7},{7,6},{8,9},{9,8},{10,11... | collective-permute-start | bytes 983048 | tf_op jit(solution)/shard_map/ppermute | solution.py:40
  50.5 5.1 %collective-permute-done.13.refs_6_ = bf16[320,512]{1,0:T(8,128)(2,1)S(1)} collective-permute-done((bf16[320,512]{1,0:T(8,128)(2,1)S(1)}, bf16[320,512]{1,0:T(8,128)(2,1)S(1)}, u32[]{:S(2)}, u32[]{:S(2)}) %collective-permute-start.13) | collective-permute-done | bytes 327712 | tf_op jit(solution)/shard_map/ppermute | solution.py:40
  57.7 3.2 %collective-permute-start.23 = (bf16[2,8,80,320]{3,2,1,0:T(8,128)(2,1)S(1)}, bf16[2,8,80,320]{3,2,1,0:T(8,128)(2,1)S(1)}, u32[]{:S(2)}, u32[]{:S(2)}) collective-permute-start(bf16[2,8,80,320]{3,2,1,0:T(8,128)(2,1)S(1)} %get-tuple-element.28), channel_id=1, source_target_pairs={{0,8},{8,0},{16,24},{24,16},{32,40},{40,32},{48,56},{56,48},{64,72... | collective-permute-start | bytes 2457608 | tf_op jit(solution)/shard_map/ppermute | solution.py:33
  61.0 3.0 %collective-permute-start.4 = (bf16[4,80,320]{2,1,0:T(8,128)(2,1)S(1)}, bf16[4,80,320]{2,1,0:T(8,128)(2,1)S(1)}, u32[]{:S(2)}, u32[]{:S(2)}) collective-permute-start(bf16[4,80,320]{2,1,0:T(8,128)(2,1)S(1)} %pad_maximum_fusion.1), channel_id=1, source_target_pairs={{0,32},{8,40},{16,48},{24,56},{32,0},{40,8},{48,16},{56,24},{64,96... | collective-permute-start | bytes 614408 | tf_op jit(solution)/shard_map/ppermute | solution.py:33
  64.0 6.3 %collective-permute-done.4 = bf16[4,80,320]{2,1,0:T(8,128)(2,1)S(1)} collective-permute-done((bf16[4,80,320]{2,1,0:T(8,128)(2,1)S(1)}, bf16[4,80,320]{2,1,0:T(8,128)(2,1)S(1)}, u32[]{:S(2)}, u32[]{:S(2)}) %collective-permute-start.4) | collective-permute-done | bytes 204832 | tf_op jit(solution)/shard_map/ppermute | solution.py:33
  71.8 10.9 %collective-permute-done.5.wy_ref = bf16[8,80,320]{2,1,0:T(8,128)(2,1)S(1)} collective-permute-done((bf16[8,80,320]{2,1,0:T(8,128)(2,1)S(1)}, bf16[8,80,320]{2,1,0:T(8,128)(2,1)S(1)}, u32[]{:S(2)}, u32[]{:S(2)}) %collective-permute-start.5) | collective-permute-done | bytes 409632 | tf_op jit(solution)/shard_map/ppermute | solution.py:33
  87.3 4.1 %collective-permute-start.18 = (bf16[320,512]{1,0:T(8,128)(2,1)S(1)}, bf16[320,512]{1,0:T(8,128)(2,1)S(1)}, u32[]{:S(2)}, u32[]{:S(2)}) collective-permute-start(bf16[320,512]{1,0:T(8,128)(2,1)S(1)} %get-tuple-element.23), channel_id=1, source_target_pairs={{0,1},{1,0},{2,3},{3,2},{4,5},{5,4},{6,7},{7,6},{8,9},{9,8},{10,11... | collective-permute-start | bytes 983048 | tf_op jit(solution)/shard_map/ppermute | solution.py:40
  92.8 4.2 %collective-permute-start.15 = (bf16[320,512]{1,0:T(8,128)(2,1)S(1)}, bf16[320,512]{1,0:T(8,128)(2,1)S(1)}, u32[]{:S(2)}, u32[]{:S(2)}) collective-permute-start(bf16[320,512]{1,0:T(8,128)(2,1)S(1)} %get-tuple-element.18), channel_id=1, source_target_pairs={{0,128},{8,136},{16,144},{24,152},{32,160},{40,168},{48,176},{56,1... | collective-permute-start | bytes 983048 | tf_op jit(solution)/shard_map/ppermute | solution.py:33
  97.0 2.2 %collective-permute-start.16 = (bf16[320,512]{1,0:T(8,128)(2,1)S(1)}, bf16[320,512]{1,0:T(8,128)(2,1)S(1)}, u32[]{:S(2)}, u32[]{:S(2)}) collective-permute-start(bf16[320,512]{1,0:T(8,128)(2,1)S(1)} %get-tuple-element.20), channel_id=1, source_target_pairs={{0,2},{1,3},{2,4},{3,5},{4,6},{5,7},{6,0},{7,1},{8,10},{9,11},{10,... | collective-permute-start | bytes 983048 | tf_op jit(solution)/shard_map/ppermute | solution.py:40
  100.9 7.0 %collective-permute-done.18 = bf16[320,512]{1,0:T(8,128)(2,1)S(1)} collective-permute-done((bf16[320,512]{1,0:T(8,128)(2,1)S(1)}, bf16[320,512]{1,0:T(8,128)(2,1)S(1)}, u32[]{:S(2)}, u32[]{:S(2)}) %collective-permute-start.18) | collective-permute-done | bytes 327712 | tf_op jit(solution)/shard_map/ppermute | solution.py:40
  108.3 8.9 %collective-permute-done.25 = bf16[4,80,320]{2,1,0:T(8,128)(2,1)S(1)} collective-permute-done((bf16[4,80,320]{2,1,0:T(8,128)(2,1)S(1)}, bf16[4,80,320]{2,1,0:T(8,128)(2,1)S(1)}, u32[]{:S(2)}, u32[]{:S(2)}) %collective-permute-start.25) | collective-permute-done | bytes 204832 | tf_op jit(solution)/shard_map/ppermute | solution.py:33
  120.6 4.3 %collective-permute-done.26 = bf16[2,80,320]{2,1,0:T(8,128)(2,1)S(1)} collective-permute-done((bf16[2,80,320]{2,1,0:T(8,128)(2,1)S(1)}, bf16[2,80,320]{2,1,0:T(8,128)(2,1)S(1)}, u32[]{:S(2)}, u32[]{:S(2)}) %collective-permute-start.26) | collective-permute-done | bytes 102432 | tf_op jit(solution)/shard_map/ppermute | solution.py:33
  125.0 4.6 %collective-permute-start.22 = (bf16[320,512]{1,0:T(8,128)(2,1)S(1)}, bf16[320,512]{1,0:T(8,128)(2,1)S(1)}, u32[]{:S(2)}, u32[]{:S(2)}) collective-permute-start(bf16[320,512]{1,0:T(8,128)(2,1)S(1)} %add_convert_fusion.1), channel_id=1, source_target_pairs={{0,1},{1,0},{2,3},{3,2},{4,5},{5,4},{6,7},{7,6},{8,9},{9,8},{10,11... | collective-permute-start | bytes 983048 | tf_op jit(solution)/shard_map/ppermute | solution.py:40
  129.7 3.1 %collective-permute-start.27 = (bf16[1,80,320]{2,1,0:T(8,128)(2,1)S(1)}, bf16[1,80,320]{2,1,0:T(8,128)(2,1)S(1)}, u32[]{:S(2)}, u32[]{:S(2)}) collective-permute-start(bf16[1,80,320]{2,1,0:T(8,128)(2,1)S(1)} %slice.57), channel_id=1, source_target_pairs={{0,128},{8,136},{16,144},{24,152},{32,160},{40,168},{48,176},{56,1... | collective-permute-start | bytes 153608 | tf_op jit(solution)/shard_map/ppermute | solution.py:33
  133.7 4.0 %collective-permute-done.27 = bf16[1,80,320]{2,1,0:T(8,128)(2,1)S(1)} collective-permute-done((bf16[1,80,320]{2,1,0:T(8,128)(2,1)S(1)}, bf16[1,80,320]{2,1,0:T(8,128)(2,1)S(1)}, u32[]{:S(2)}, u32[]{:S(2)}) %collective-permute-start.27) | collective-permute-done | bytes 51232 | tf_op jit(solution)/shard_map/ppermute | solution.py:33
  137.8 7.7 %shard_map.77 = bf16[3,320,512]{2,1,0:T(8,128)(2,1)} custom-call(s32[1]{0:T(128)S(6)} %copy.8.count_ref, bf16[3,320,512]{2,1,0:T(8,128)(2,1)S(1)} %bitcast.28, bf16[320,512]{1,0:T(8,128)(2,1)S(1)} %get-tuple-element.19.refs_0_, bf16[320,512]{1,0:T(8,128)(2,1)S(1)} %collective-permute-done.16.refs_1_, bf16[320,512]{1,0:T(8,128)(2,1)S(1)} %collective-permute-done.17.refs_2_, ...), custom_call_target="tpu_custom_call" | custom-call | flops 1006632960 | bytes 2621440 | tf_op jit(solution)/shard_map/pallas_call | solution.py:117
  (64 shorter events, 21.0 us)
Async XLA Ops:
  6.3 36.0 %collective-permute-start.11 = (bf16[320,512]{1,0:T(8,128)(2,1)S(1)}, bf16[320,512]{1,0:T(8,128)(2,1)S(1)}, u32[]{:S(2)}, u32[]{:S(2)}) collective-permute-start(bf16[320,512]{1,0:T(8,128)(2,1)S(1)} %shard_map.76.refs_0_), channel_id=1, source_target_pairs={{0,1},{1,0},{2,3},{3,2},{4,5},{5,4},{6,7},{7,6},{8,9},{9,8},{10,11... | collective-permute-start | bytes 983048 | tf_op jit(solution)/shard_map/ppermute | solution.py:40
  10.2 33.2 %collective-permute-start = (bf16[320,512]{1,0:T(8,128)(2,1)S(1)}, bf16[320,512]{1,0:T(8,128)(2,1)S(1)}, u32[]{:S(2)}, u32[]{:S(2)}) collective-permute-start(bf16[320,512]{1,0:T(8,128)(2,1)S(1)} %slice_bitcast_fusion.1), channel_id=1, source_target_pairs={{0,128},{8,136},{16,144},{24,152},{32,160},{40,168},{48,176},{56,1... | collective-permute-start | bytes 983048 | tf_op jit(solution)/shard_map/ppermute | solution.py:33
  17.2 26.7 %collective-permute-start.10 = (bf16[320,512]{1,0:T(8,128)(2,1)S(1)}, bf16[320,512]{1,0:T(8,128)(2,1)S(1)}, u32[]{:S(2)}, u32[]{:S(2)}) collective-permute-start(bf16[320,512]{1,0:T(8,128)(2,1)S(1)} %shard_map.76.refs_0_), channel_id=1, source_target_pairs={{0,4},{1,5},{2,6},{3,7},{4,0},{5,1},{6,2},{7,3},{8,12},{9,13},{10,... | collective-permute-start | bytes 983048 | tf_op jit(solution)/shard_map/ppermute | solution.py:40
  19.9 30.1 %collective-permute-start.8 = (bf16[320,512]{1,0:T(8,128)(2,1)S(1)}, bf16[320,512]{1,0:T(8,128)(2,1)S(1)}, u32[]{:S(2)}, u32[]{:S(2)}) collective-permute-start(bf16[320,512]{1,0:T(8,128)(2,1)S(1)} %shard_map.76.refs_0_), channel_id=1, source_target_pairs={{0,6},{1,7},{2,0},{3,1},{4,2},{5,3},{6,4},{7,5},{8,14},{9,15},{10,... | collective-permute-start | bytes 983048 | tf_op jit(solution)/shard_map/ppermute | solution.py:40
  28.4 8.6 %collective-permute-start.2 = (bf16[1,80,320]{2,1,0:T(8,128)(2,1)S(1)}, bf16[1,80,320]{2,1,0:T(8,128)(2,1)S(1)}, u32[]{:S(2)}, u32[]{:S(2)}) collective-permute-start(bf16[1,80,320]{2,1,0:T(8,128)(2,1)S(1)} %bitcast.31), channel_id=1, source_target_pairs={{0,128},{8,136},{16,144},{24,152},{32,160},{40,168},{48,176},{56,1... | collective-permute-start | bytes 153608 | tf_op jit(solution)/shard_map/ppermute | solution.py:33
  37.0 13.4 %collective-permute-start.9 = (bf16[320,512]{1,0:T(8,128)(2,1)S(1)}, bf16[320,512]{1,0:T(8,128)(2,1)S(1)}, u32[]{:S(2)}, u32[]{:S(2)}) collective-permute-start(bf16[320,512]{1,0:T(8,128)(2,1)S(1)} %shard_map.76.refs_0_), channel_id=1, source_target_pairs={{0,2},{1,3},{2,4},{3,5},{4,6},{5,7},{6,0},{7,1},{8,10},{9,11},{10,... | collective-permute-start | bytes 983048 | tf_op jit(solution)/shard_map/ppermute | solution.py:40
  42.4 8.1 %collective-permute-start.12 = (bf16[320,512]{1,0:T(8,128)(2,1)S(1)}, bf16[320,512]{1,0:T(8,128)(2,1)S(1)}, u32[]{:S(2)}, u32[]{:S(2)}) collective-permute-start(bf16[320,512]{1,0:T(8,128)(2,1)S(1)} %collective-permute-done.11.refs_4_), channel_id=1, source_target_pairs={{0,6},{1,7},{2,0},{3,1},{4,2},{5,3},{6,4},{7,5},{8,14},{9,15},{10,... | collective-permute-start | bytes 983048 | tf_op jit(solution)/shard_map/ppermute | solution.py:40
  43.4 12.2 %collective-permute-start.13 = (bf16[320,512]{1,0:T(8,128)(2,1)S(1)}, bf16[320,512]{1,0:T(8,128)(2,1)S(1)}, u32[]{:S(2)}, u32[]{:S(2)}) collective-permute-start(bf16[320,512]{1,0:T(8,128)(2,1)S(1)} %collective-permute-done.11.refs_4_), channel_id=1, source_target_pairs={{0,2},{1,3},{2,4},{3,5},{4,6},{5,7},{6,0},{7,1},{8,10},{9,11},{10,... | collective-permute-start | bytes 983048 | tf_op jit(solution)/shard_map/ppermute | solution.py:40
  43.8 12.1 %collective-permute-start.14 = (bf16[320,512]{1,0:T(8,128)(2,1)S(1)}, bf16[320,512]{1,0:T(8,128)(2,1)S(1)}, u32[]{:S(2)}, u32[]{:S(2)}) collective-permute-start(bf16[320,512]{1,0:T(8,128)(2,1)S(1)} %collective-permute-done.10.refs_3_), channel_id=1, source_target_pairs={{0,1},{1,0},{2,3},{3,2},{4,5},{5,4},{6,7},{7,6},{8,9},{9,8},{10,11... | collective-permute-start | bytes 983048 | tf_op jit(solution)/shard_map/ppermute | solution.py:40
  50.1 10.9 %collective-permute-start.3 = (bf16[2,80,320]{2,1,0:T(8,128)(2,1)S(1)}, bf16[2,80,320]{2,1,0:T(8,128)(2,1)S(1)}, u32[]{:S(2)}, u32[]{:S(2)}) collective-permute-start(bf16[2,80,320]{2,1,0:T(8,128)(2,1)S(1)} %pad_maximum_fusion.2), channel_id=1, source_target_pairs={{0,64},{8,72},{16,80},{24,88},{32,96},{40,104},{48,112},{56,120},{... | collective-permute-start | bytes 307208 | tf_op jit(solution)/shard_map/ppermute | solution.py:33
  57.7 26.4 %collective-permute-start.23 = (bf16[2,8,80,320]{3,2,1,0:T(8,128)(2,1)S(1)}, bf16[2,8,80,320]{3,2,1,0:T(8,128)(2,1)S(1)}, u32[]{:S(2)}, u32[]{:S(2)}) collective-permute-start(bf16[2,8,80,320]{3,2,1,0:T(8,128)(2,1)S(1)} %get-tuple-element.28), channel_id=1, source_target_pairs={{0,8},{8,0},{16,24},{24,16},{32,40},{40,32},{48,56},{56,48},{64,72... | collective-permute-start | bytes 2457608 | tf_op jit(solution)/shard_map/ppermute | solution.py:33
  61.0 9.3 %collective-permute-start.4 = (bf16[4,80,320]{2,1,0:T(8,128)(2,1)S(1)}, bf16[4,80,320]{2,1,0:T(8,128)(2,1)S(1)}, u32[]{:S(2)}, u32[]{:S(2)}) collective-permute-start(bf16[4,80,320]{2,1,0:T(8,128)(2,1)S(1)} %pad_maximum_fusion.1), channel_id=1, source_target_pairs={{0,32},{8,40},{16,48},{24,56},{32,0},{40,8},{48,16},{56,24},{64,96... | collective-permute-start | bytes 614408 | tf_op jit(solution)/shard_map/ppermute | solution.py:33
  70.4 12.3 %collective-permute-start.5 = (bf16[8,80,320]{2,1,0:T(8,128)(2,1)S(1)}, bf16[8,80,320]{2,1,0:T(8,128)(2,1)S(1)}, u32[]{:S(2)}, u32[]{:S(2)}) collective-permute-start(bf16[8,80,320]{2,1,0:T(8,128)(2,1)S(1)} %pad_maximum_fusion.w0_ref), channel_id=1, source_target_pairs={{0,16},{8,24},{16,0},{24,8},{32,48},{40,56},{48,32},{56,40},{64,80... | collective-permute-start | bytes 1228808 | tf_op jit(solution)/shard_map/ppermute | solution.py:33
  70.9 13.9 %collective-permute-start.6 = (bf16[8,80,320]{2,1,0:T(8,128)(2,1)S(1)}, bf16[8,80,320]{2,1,0:T(8,128)(2,1)S(1)}, u32[]{:S(2)}, u32[]{:S(2)}) collective-permute-start(bf16[8,80,320]{2,1,0:T(8,128)(2,1)S(1)} %pad_maximum_fusion.w0_ref), channel_id=1, source_target_pairs={{0,8},{8,0},{16,24},{24,16},{32,40},{40,32},{48,56},{56,48},{64,72... | collective-permute-start | bytes 1228808 | tf_op jit(solution)/shard_map/ppermute | solution.py:33
  84.2 15.5 %collective-permute-start.24 = (bf16[8,80,320]{2,1,0:T(8,128)(2,1)S(1)}, bf16[8,80,320]{2,1,0:T(8,128)(2,1)S(1)}, u32[]{:S(2)}, u32[]{:S(2)}) collective-permute-start(bf16[8,80,320]{2,1,0:T(8,128)(2,1)S(1)} %fusion.1), channel_id=1, source_target_pairs={{0,16},{8,24},{16,0},{24,8},{32,48},{40,56},{48,32},{56,40},{64,80... | collective-permute-start | bytes 1228808 | tf_op jit(solution)/shard_map/ppermute | solution.py:33
  87.3 20.6 %collective-permute-start.18 = (bf16[320,512]{1,0:T(8,128)(2,1)S(1)}, bf16[320,512]{1,0:T(8,128)(2,1)S(1)}, u32[]{:S(2)}, u32[]{:S(2)}) collective-permute-start(bf16[320,512]{1,0:T(8,128)(2,1)S(1)} %get-tuple-element.23), channel_id=1, source_target_pairs={{0,1},{1,0},{2,3},{3,2},{4,5},{5,4},{6,7},{7,6},{8,9},{9,8},{10,11... | collective-permute-start | bytes 983048 | tf_op jit(solution)/shard_map/ppermute | solution.py:40
  92.8 36.8 %collective-permute-start.15 = (bf16[320,512]{1,0:T(8,128)(2,1)S(1)}, bf16[320,512]{1,0:T(8,128)(2,1)S(1)}, u32[]{:S(2)}, u32[]{:S(2)}) collective-permute-start(bf16[320,512]{1,0:T(8,128)(2,1)S(1)} %get-tuple-element.18), channel_id=1, source_target_pairs={{0,128},{8,136},{16,144},{24,152},{32,160},{40,168},{48,176},{56,1... | collective-permute-start | bytes 983048 | tf_op jit(solution)/shard_map/ppermute | solution.py:33
  97.0 40.7 %collective-permute-start.16 = (bf16[320,512]{1,0:T(8,128)(2,1)S(1)}, bf16[320,512]{1,0:T(8,128)(2,1)S(1)}, u32[]{:S(2)}, u32[]{:S(2)}) collective-permute-start(bf16[320,512]{1,0:T(8,128)(2,1)S(1)} %get-tuple-element.20), channel_id=1, source_target_pairs={{0,2},{1,3},{2,4},{3,5},{4,6},{5,7},{6,0},{7,1},{8,10},{9,11},{10,... | collective-permute-start | bytes 983048 | tf_op jit(solution)/shard_map/ppermute | solution.py:40
  99.2 18.0 %collective-permute-start.21 = (bf16[320,512]{1,0:T(8,128)(2,1)S(1)}, bf16[320,512]{1,0:T(8,128)(2,1)S(1)}, u32[]{:S(2)}, u32[]{:S(2)}) collective-permute-start(bf16[320,512]{1,0:T(8,128)(2,1)S(1)} %get-tuple-element.26), channel_id=1, source_target_pairs={{0,6},{1,7},{2,0},{3,1},{4,2},{5,3},{6,4},{7,5},{8,14},{9,15},{10,... | collective-permute-start | bytes 983048 | tf_op jit(solution)/shard_map/ppermute | solution.py:40
  99.7 19.0 %collective-permute-start.20 = (bf16[320,512]{1,0:T(8,128)(2,1)S(1)}, bf16[320,512]{1,0:T(8,128)(2,1)S(1)}, u32[]{:S(2)}, u32[]{:S(2)}) collective-permute-start(bf16[320,512]{1,0:T(8,128)(2,1)S(1)} %get-tuple-element.25), channel_id=1, source_target_pairs={{0,2},{1,3},{2,4},{3,5},{4,6},{5,7},{6,0},{7,1},{8,10},{9,11},{10,... | collective-permute-start | bytes 983048 | tf_op jit(solution)/shard_map/ppermute | solution.py:40
  107.9 9.3 %collective-permute-start.25 = (bf16[4,80,320]{2,1,0:T(8,128)(2,1)S(1)}, bf16[4,80,320]{2,1,0:T(8,128)(2,1)S(1)}, u32[]{:S(2)}, u32[]{:S(2)}) collective-permute-start(bf16[4,80,320]{2,1,0:T(8,128)(2,1)S(1)} %slice.53), channel_id=1, source_target_pairs={{0,32},{8,40},{16,48},{24,56},{32,0},{40,8},{48,16},{56,24},{64,96... | collective-permute-start | bytes 614408 | tf_op jit(solution)/shard_map/ppermute | solution.py:33
  117.2 20.6 %collective-permute-start.17 = (bf16[320,512]{1,0:T(8,128)(2,1)S(1)}, bf16[320,512]{1,0:T(8,128)(2,1)S(1)}, u32[]{:S(2)}, u32[]{:S(2)}) collective-permute-start(bf16[320,512]{1,0:T(8,128)(2,1)S(1)} %get-tuple-element.21), channel_id=1, source_target_pairs={{0,6},{1,7},{2,0},{3,1},{4,2},{5,3},{6,4},{7,5},{8,14},{9,15},{10,... | collective-permute-start | bytes 983048 | tf_op jit(solution)/shard_map/ppermute | solution.py:40
  117.3 20.5 %collective-permute-start.19 = (bf16[320,512]{1,0:T(8,128)(2,1)S(1)}, bf16[320,512]{1,0:T(8,128)(2,1)S(1)}, u32[]{:S(2)}, u32[]{:S(2)}) collective-permute-start(bf16[320,512]{1,0:T(8,128)(2,1)S(1)} %add_convert_fusion.2), channel_id=1, source_target_pairs={{0,4},{1,5},{2,6},{3,7},{4,0},{5,1},{6,2},{7,3},{8,12},{9,13},{10,... | collective-permute-start | bytes 983048 | tf_op jit(solution)/shard_map/ppermute | solution.py:40
  125.0 12.8 %collective-permute-start.22 = (bf16[320,512]{1,0:T(8,128)(2,1)S(1)}, bf16[320,512]{1,0:T(8,128)(2,1)S(1)}, u32[]{:S(2)}, u32[]{:S(2)}) collective-permute-start(bf16[320,512]{1,0:T(8,128)(2,1)S(1)} %add_convert_fusion.1), channel_id=1, source_target_pairs={{0,1},{1,0},{2,3},{3,2},{4,5},{5,4},{6,7},{7,6},{8,9},{9,8},{10,11... | collective-permute-start | bytes 983048 | tf_op jit(solution)/shard_map/ppermute | solution.py:40
  (9 other events, 80.5 us)

commit v3 on v2

--- a/solution.py
+++ b/solution.py
@@ -66,7 +66,7 @@
 def stack_index(steps):
     z = lax.axis_index("dp") // 4
     apart = lax.rem(lax.axis_index("tensor") + steps, Z) ^ z
-    return lax.rem(apart, 2) * 4 + lax.rem(apart // 2, 2) * 2 + apart // 4
+    return lax.rem(apart, 4) * 2 + apart // 4
 
 
 def column_of(flip_y, flip_c):
@@ -91,8 +91,8 @@
     ctx_ref[...] = jnp.where(live, context, 0.0).astype(BF16)
 
 
-def backward_kernel(count_ref, qkv_ref, *refs):
-    grad_refs, out_ref = refs[:-1], refs[-1]
+def backward_kernel(skipped, count_ref, *refs):
+    qkv_ref, grad_refs, out_ref = refs[skipped], refs[skipped + 1 : -1], refs[-1]
     count = count_ref[0]
     grad = functools.reduce(lambda a, b: a + b, [r[...].astype(F32) for r in grad_refs])
     live = lax.broadcasted_iota(jnp.int32, (1, grad.shape[1]), 1) < count
@@ -108,27 +108,48 @@
     out_ref[1] = dot(q, grad_scores, 1, 1).astype(BF16)
 
 
-def heads_call(kernel, count, qkv, grads, out_planes):
+def kernel_cost(dots, heads, length):
+    return pl.CostEstimate(
+        flops=2 * dots * heads * HEAD_DIM * length * length,
+        bytes_accessed=8 * heads * HEAD_DIM * length * 2,
+        transcendentals=heads * length * length,
+    )
+
+
+def forward(count, qkv):
     _, columns, length = qkv.shape
     heads = columns // HEAD_DIM
-    plane = pl.BlockSpec((HEAD_DIM, length), lambda h: (h, 0))
-    planes = pl.BlockSpec((3, HEAD_DIM, length), lambda h: (0, h, 0))
-    dots = 6 if out_planes else 2
-    return pl.pallas_call(
-        kernel,
+    return pl.pallas_call(
+        forward_kernel,
+        name="forward",
         grid=(heads,),
-        in_specs=[SMEM, planes] + [plane] * len(grads),
-        out_specs=planes if out_planes else plane,
-        out_shape=jax.ShapeDtypeStruct(
-            (3, columns, length) if out_planes else (columns, length), BF16
-        ),
-        compiler_params=pltpu.CompilerParams(vmem_limit_bytes=16 << 20),
-        cost_estimate=pl.CostEstimate(
-            flops=2 * dots * columns * length * length,
-            bytes_accessed=8 * columns * length * 2,
-            transcendentals=heads * length * length,
-        ),
-    )(count, qkv, *grads)
+        in_specs=[SMEM, pl.BlockSpec((3, HEAD_DIM, length), lambda h: (0, h, 0))],
+        out_specs=pl.BlockSpec((HEAD_DIM, length), lambda h: (h, 0)),
+        out_shape=jax.ShapeDtypeStruct((columns, length), BF16),
+        compiler_params=pltpu.CompilerParams(vmem_limit_bytes=16 << 20),
+        cost_estimate=kernel_cost(2, heads, length),
+    )(count, qkv)
+
+
+def backward(count, qkv, grads, first, heads, earlier=None):
+    length = qkv.shape[2]
+    plane = pl.BlockSpec((HEAD_DIM, length), lambda h: (h + first, 0))
+    planes = pl.BlockSpec((3, HEAD_DIM, length), lambda h: (0, h + first, 0))
+    before = [] if earlier is None else [earlier]
+    return pl.pallas_call(
+        functools.partial(backward_kernel, len(before)),
+        name="backward",
+        grid=(heads,),
+        in_specs=[SMEM]
+        + [pl.BlockSpec(memory_space=pl.ANY)] * len(before)
+        + [planes]
+        + [plane] * len(grads),
+        out_specs=planes,
+        out_shape=jax.ShapeDtypeStruct(qkv.shape, BF16),
+        input_output_aliases={1: 0} if before else {},
+        compiler_params=pltpu.CompilerParams(vmem_limit_bytes=16 << 20),
+        cost_estimate=kernel_cost(6, heads, length),
+    )(count, *before, qkv, *grads)
 
 
 def grad_partial_kernel(cot_ref, w0_ref, wy_ref, wc_ref, wcy_ref, all_ref, *out_refs):
@@ -226,9 +247,11 @@
 
     pairs = swap_pairs()
     moved = swapped(out_weight.T, pairs)
+
+    ctx = forward(residue_counts, qkv)
+
+    cot_slots, ctx = lax.optimization_barrier((cot_slots, ctx))
     guest_cot = half_round(cot_slots[1])
-
-    ctx = heads_call(forward_kernel, residue_counts, qkv, (), False)
 
     block = {(0, 0): ctx}
     block[0, 1] = along_tensor(ctx, 0, 1)
@@ -240,10 +263,8 @@
     block[2, 1] = along_tensor(block[2, 0], 0, 1)
     blocks = [block[place] for place in PLACES]
 
-    stack = moved[None]
-    for bit in (4, 2, 1):
-        stack = jnp.concatenate([stack, exchanged(stack, 4 * bit)])
-    w0 = stack
+    two = jnp.stack([moved, exchanged(moved, 16)])
+    w0 = jnp.concatenate([two] + [exchanged(two, 4 * far) for far in (1, 2, 3)])
     wy = exchanged(w0, 2)
     wc = exchanged(w0, 1)
     wcy = exchanged(wy, 1)
@@ -262,17 +283,21 @@
     keep, send = weight_partial(cot, blocks)
     both = exchanged(send, 1)
     total = added(keep[0], both[0], exchanged(added(keep[1], both[1]), 2))
-    for bit in (1, 2, 4):
-        half = total.shape[0] // 2
-        total = added(total[:half], exchanged(total[half:], 4 * bit))
+    terms = [exchanged(total[2 * far : 2 * far + 2], 4 * far) for far in (1, 2, 3)]
+    total = added(total[:2], *terms)
+    total = added(total[0], exchanged(total[1], 16))
     home_pairs = [(there, here) for here, there in pairs]
-    grad_weight = swapped(total[0], home_pairs).astype(F32).T
+    grad_weight = swapped(total, home_pairs).astype(F32).T
 
     home, guest = layer_out_of(migrate_plan, weight, blocks)
     returned = half_round(guest)
     layer_out = jnp.transpose(jnp.stack([home, returned]), (0, 2, 1))
 
-    grad_qkv = heads_call(backward_kernel, residue_counts, qkv, (part[0, 0], *got), True)
+    grads = (part[0, 0], *got)
+    heads = qkv.shape[1] // HEAD_DIM
+    early = heads - heads // 2
+    grad_qkv = backward(residue_counts, qkv, grads, 0, early)
+    grad_qkv = backward(residue_counts, qkv, grads, early, heads - early, grad_qkv)
     return layer_out, jnp.transpose(grad_qkv, (0, 2, 1)), grad_weight
 
 

time: 149 us -> 150 us (level); the launches traced: 146 us -> 149 us
  starting transfers between devices: 64.6 us -> 67.7 us
    ppermute x14, starting transfers between devices: 34.2 us -> 19.7 us  [along_tensor(): return lax.ppermute(value, 'tensor', [(i, to(i)) for i in range(N_TENSOR)])]
    ppermute x2, starting transfers between devices: 0.18 us -> 9.52 us  [swapped(): return lax.ppermute(value, ('dp', 'tensor'), pairs)]
    ppermute x13 -> x15, starting transfers between devices: 30.2 us -> 38.5 us  [along_dp(): return lax.ppermute(value, 'dp', [(i, to(i)) for i in range(N_DP)])]
    ppermute x2, waiting for transfers between devices: 7.54 us -> 0.01 us  [swapped(): return lax.ppermute(value, ('dp', 'tensor'), pairs)]
    ppermute x13 -> x15, waiting for transfers between devices: 39.2 us -> 44.9 us  [along_dp(): return lax.ppermute(value, 'dp', [(i, to(i)) for i in range(N_DP)])]
    pallas_call x2 -> x3, Pallas kernels: 11.6 us -> 12.3 us  [the longest x2 8.43 us: backward(): pl.pallas_call(functools.partial(backward_kernel, len(before)), name='bac...]
  transfers between devices with their start and end apart: 29 -> 31, of which waited for: 11 -> 13; matrix products, arithmetic and copies ran while one was open for 1% -> 1% of each run, Pallas kernels for 9% -> 9%
where the time goes in v3:
time: 150 us; the launch traced here: 149 us
  starting transfers between devices  67.7 us (45%)
  waiting for transfers between devices  58.7 us (39%)
  Pallas kernels  17.2 us (11%)
  other arithmetic  2.22 us (1%)
  between operations  2.13 us (1%)
    ppermute x15, waiting for transfers between devices, along_dp(): return lax.ppermute(value, 'dp', [(i, to(i)) for i in range(N_DP)])  44.9 us
    ppermute x15, starting transfers between devices, along_dp(): return lax.ppermute(value, 'dp', [(i, to(i)) for i in range(N_DP)])  38.5 us
    ppermute x14, starting transfers between devices, along_tensor(): return lax.ppermute(value, 'tensor', [(i, to(i)) for i in range(N_TENSOR)])  19.7 us
    ppermute x14, waiting for transfers between devices, along_tensor(): return lax.ppermute(value, 'tensor', [(i, to(i)) for i in range(N_TENSOR)])  13.7 us
    ppermute x2, starting transfers between devices, swapped(): return lax.ppermute(value, ('dp', 'tensor'), pairs)  9.52 us
    pallas_call x2, Pallas kernels, backward(): pl.pallas_call(functools.partial(backward_kernel, len(before)), name='bac...  8.43 us
    pallas_call x1, Pallas kernels, forward(): pl.pallas_call(forward_kernel, name='forward', grid=(heads,), in_specs=[S...  3.82 us
  transfers between devices with their start and end apart: 31, of which 13 were waited for; matrix products, arithmetic and copies ran while one was open for 1% of the time, Pallas kernels for 9%

profile of v3, /device:TPU:1, one launch (start us, length us, event | category | flops | bytes accessed | tf_op | source)
XLA Modules:
  0.0 149.3 jit_solution(2356219167019392203)
XLA Ops:
  2.5 3.8 %forward.1.refs_0_ = bf16[320,512]{1,0:T(8,128)(2,1)S(1)} custom-call(s32[1]{0:T(128)S(6)} %copy.14.count_ref, bf16[3,320,512]{2,1,0:T(8,128)(2,1)S(1)} %bitcast.32), custom_call_target="tpu_custom_call" | custom-call | flops 335544320 | bytes 2621440 | tf_op jit(solution)/shard_map/forward/pallas_call | solution.py:122
  6.3 3.4 %collective-permute-start.9 = (bf16[320,512]{1,0:T(8,128)(2,1)S(1)}, bf16[320,512]{1,0:T(8,128)(2,1)S(1)}, u32[]{:S(2)}, u32[]{:S(2)}) collective-permute-start(bf16[320,512]{1,0:T(8,128)(2,1)S(1)} %forward.1.refs_0_), channel_id=1, source_target_pairs={{0,6},{1,7},{2,0},{3,1},{4,2},{5,3},{6,4},{7,5},{8,14},{9,15},{10,... | collective-permute-start | bytes 983048 | tf_op jit(solution)/shard_map/ppermute | solution.py:40
  10.2 2.9 %collective-permute-start.12 = (bf16[320,512]{1,0:T(8,128)(2,1)S(1)}, bf16[320,512]{1,0:T(8,128)(2,1)S(1)}, u32[]{:S(2)}, u32[]{:S(2)}) collective-permute-start(bf16[320,512]{1,0:T(8,128)(2,1)S(1)} %forward.1.refs_0_), channel_id=1, source_target_pairs={{0,1},{1,0},{2,3},{3,2},{4,5},{5,4},{6,7},{7,6},{8,9},{9,8},{10,11... | collective-permute-start | bytes 983048 | tf_op jit(solution)/shard_map/ppermute | solution.py:40
  13.1 6.9 %collective-permute-start.1 = (bf16[80,320]{1,0:T(8,128)(2,1)S(1)}, bf16[80,320]{1,0:T(8,128)(2,1)S(1)}, u32[]{:S(2)}, u32[]{:S(2)}) collective-permute-start(bf16[80,320]{1,0:T(8,128)(2,1)S(1)} %bitcast.42), channel_id=1, source_target_pairs={{0,128},{2,96},{6,160},{4,64},{1,192},{3,32},{7,224},{5,0},{8,136}... | collective-permute-start | bytes 153608 | tf_op jit(solution)/shard_map/ppermute | solution.py:55
  20.1 3.4 %collective-permute-start = (bf16[320,512]{1,0:T(8,128)(2,1)S(1)}, bf16[320,512]{1,0:T(8,128)(2,1)S(1)}, u32[]{:S(2)}, u32[]{:S(2)}) collective-permute-start(bf16[320,512]{1,0:T(8,128)(2,1)S(1)} %slice_bitcast_fusion), channel_id=1, source_target_pairs={{0,128},{8,136},{16,144},{24,152},{32,160},{40,168},{48,176},{56,1... | collective-permute-start | bytes 983048 | tf_op jit(solution)/shard_map/ppermute | solution.py:33
  24.2 3.6 %collective-permute-start.2 = (bf16[80,320]{1,0:T(8,128)(2,1)S(1)}, bf16[80,320]{1,0:T(8,128)(2,1)S(1)}, u32[]{:S(2)}, u32[]{:S(2)}) collective-permute-start(bf16[80,320]{1,0:T(8,128)(2,1)S(1)} %collective-permute-done.1), channel_id=1, source_target_pairs={{0,128},{8,136},{16,144},{24,152},{32,160},{40,168},{48,176},{56,1... | collective-permute-start | bytes 153608 | tf_op jit(solution)/shard_map/ppermute | solution.py:33
  27.8 13.5 %collective-permute-done.2 = bf16[80,320]{1,0:T(8,128)(2,1)S(1)} collective-permute-done((bf16[80,320]{1,0:T(8,128)(2,1)S(1)}, bf16[80,320]{1,0:T(8,128)(2,1)S(1)}, u32[]{:S(2)}, u32[]{:S(2)}) %collective-permute-start.2) | collective-permute-done | bytes 51232 | tf_op jit(solution)/shard_map/ppermute | solution.py:33
  41.4 3.7 %collective-permute-done.3 = bf16[2,80,320]{2,1,0:T(8,128)(2,1)S(1)} collective-permute-done((bf16[2,80,320]{2,1,0:T(8,128)(2,1)S(1)}, bf16[2,80,320]{2,1,0:T(8,128)(2,1)S(1)}, u32[]{:S(2)}, u32[]{:S(2)}) %collective-permute-start.3) | collective-permute-done | bytes 102432 | tf_op jit(solution)/shard_map/ppermute | solution.py:33
  45.1 6.6 %collective-permute-start.4 = (bf16[2,80,320]{2,1,0:T(8,128)(2,1)S(1)}, bf16[2,80,320]{2,1,0:T(8,128)(2,1)S(1)}, u32[]{:S(2)}, u32[]{:S(2)}) collective-permute-start(bf16[2,80,320]{2,1,0:T(8,128)(2,1)S(1)} %pad_maximum_fusion), channel_id=1, source_target_pairs={{0,64},{8,72},{16,80},{24,88},{32,96},{40,104},{48,112},{56,120},{... | collective-permute-start | bytes 307208 | tf_op jit(solution)/shard_map/ppermute | solution.py:33
  51.7 3.6 %collective-permute-done.4 = bf16[2,80,320]{2,1,0:T(8,128)(2,1)S(1)} collective-permute-done((bf16[2,80,320]{2,1,0:T(8,128)(2,1)S(1)}, bf16[2,80,320]{2,1,0:T(8,128)(2,1)S(1)}, u32[]{:S(2)}, u32[]{:S(2)}) %collective-permute-start.4) | collective-permute-done | bytes 102432 | tf_op jit(solution)/shard_map/ppermute | solution.py:33
  55.3 2.8 %collective-permute-start.5 = (bf16[2,80,320]{2,1,0:T(8,128)(2,1)S(1)}, bf16[2,80,320]{2,1,0:T(8,128)(2,1)S(1)}, u32[]{:S(2)}, u32[]{:S(2)}) collective-permute-start(bf16[2,80,320]{2,1,0:T(8,128)(2,1)S(1)} %pad_maximum_fusion), channel_id=1, source_target_pairs={{0,96},{8,104},{16,112},{24,120},{32,64},{40,72},{48,80},{56,88},{... | collective-permute-start | bytes 307208 | tf_op jit(solution)/shard_map/ppermute | solution.py:33
  58.1 2.9 %collective-permute-done.5 = bf16[2,80,320]{2,1,0:T(8,128)(2,1)S(1)} collective-permute-done((bf16[2,80,320]{2,1,0:T(8,128)(2,1)S(1)}, bf16[2,80,320]{2,1,0:T(8,128)(2,1)S(1)}, u32[]{:S(2)}, u32[]{:S(2)}) %collective-permute-start.5) | collective-permute-done | bytes 102432 | tf_op jit(solution)/shard_map/ppermute | solution.py:33
  61.0 2.7 %collective-permute-start.13 = (bf16[320,512]{1,0:T(8,128)(2,1)S(1)}, bf16[320,512]{1,0:T(8,128)(2,1)S(1)}, u32[]{:S(2)}, u32[]{:S(2)}) collective-permute-start(bf16[320,512]{1,0:T(8,128)(2,1)S(1)} %collective-permute-done.12.refs_4_), channel_id=1, source_target_pairs={{0,6},{1,7},{2,0},{3,1},{4,2},{5,3},{6,4},{7,5},{8,14},{9,15},{10,... | collective-permute-start | bytes 983048 | tf_op jit(solution)/shard_map/ppermute | solution.py:40
  65.3 2.8 %collective-permute-done.10.refs_2_ = bf16[320,512]{1,0:T(8,128)(2,1)S(1)} collective-permute-done((bf16[320,512]{1,0:T(8,128)(2,1)S(1)}, bf16[320,512]{1,0:T(8,128)(2,1)S(1)}, u32[]{:S(2)}, u32[]{:S(2)}) %collective-permute-start.10) | collective-permute-done | bytes 327712 | tf_op jit(solution)/shard_map/ppermute | solution.py:40
  68.1 3.5 %collective-permute-done.14.refs_6_ = bf16[320,512]{1,0:T(8,128)(2,1)S(1)} collective-permute-done((bf16[320,512]{1,0:T(8,128)(2,1)S(1)}, bf16[320,512]{1,0:T(8,128)(2,1)S(1)}, u32[]{:S(2)}, u32[]{:S(2)}) %collective-permute-start.14) | collective-permute-done | bytes 327712 | tf_op jit(solution)/shard_map/ppermute | solution.py:40
  73.4 11.6 %collective-permute-start.24 = (bf16[2,8,80,320]{3,2,1,0:T(8,128)(2,1)S(1)}, bf16[2,8,80,320]{3,2,1,0:T(8,128)(2,1)S(1)}, u32[]{:S(2)}, u32[]{:S(2)}) collective-permute-start(bf16[2,8,80,320]{3,2,1,0:T(8,128)(2,1)S(1)} %get-tuple-element.32), channel_id=1, source_target_pairs={{0,8},{8,0},{16,24},{24,16},{32,40},{40,32},{48,56},{56,48},{64,72... | collective-permute-start | bytes 2457608 | tf_op jit(solution)/shard_map/ppermute | solution.py:33
  90.3 2.9 %collective-permute-start.22 = (bf16[320,512]{1,0:T(8,128)(2,1)S(1)}, bf16[320,512]{1,0:T(8,128)(2,1)S(1)}, u32[]{:S(2)}, u32[]{:S(2)}) collective-permute-start(bf16[320,512]{1,0:T(8,128)(2,1)S(1)} %get-tuple-element.30), channel_id=1, source_target_pairs={{0,6},{1,7},{2,0},{3,1},{4,2},{5,3},{6,4},{7,5},{8,14},{9,15},{10,... | collective-permute-start | bytes 983048 | tf_op jit(solution)/shard_map/ppermute | solution.py:40
  96.1 5.3 %collective-permute-start.16 = (bf16[320,512]{1,0:T(8,128)(2,1)S(1)}, bf16[320,512]{1,0:T(8,128)(2,1)S(1)}, u32[]{:S(2)}, u32[]{:S(2)}) collective-permute-start(bf16[320,512]{1,0:T(8,128)(2,1)S(1)} %get-tuple-element.22), channel_id=1, source_target_pairs={{0,128},{8,136},{16,144},{24,152},{32,160},{40,168},{48,176},{56,1... | collective-permute-start | bytes 983048 | tf_op jit(solution)/shard_map/ppermute | solution.py:33
  107.0 7.4 %collective-permute-done.19 = bf16[320,512]{1,0:T(8,128)(2,1)S(1)} collective-permute-done((bf16[320,512]{1,0:T(8,128)(2,1)S(1)}, bf16[320,512]{1,0:T(8,128)(2,1)S(1)}, u32[]{:S(2)}, u32[]{:S(2)}) %collective-permute-start.19) | collective-permute-done | bytes 327712 | tf_op jit(solution)/shard_map/ppermute | solution.py:40
  114.5 3.5 %collective-permute-done.28 = bf16[2,80,320]{2,1,0:T(8,128)(2,1)S(1)} collective-permute-done((bf16[2,80,320]{2,1,0:T(8,128)(2,1)S(1)}, bf16[2,80,320]{2,1,0:T(8,128)(2,1)S(1)}, u32[]{:S(2)}, u32[]{:S(2)}) %collective-permute-start.28) | collective-permute-done | bytes 102432 | tf_op jit(solution)/shard_map/ppermute | solution.py:33
  118.8 8.4 %collective-permute-done.27 = bf16[2,80,320]{2,1,0:T(8,128)(2,1)S(1)} collective-permute-done((bf16[2,80,320]{2,1,0:T(8,128)(2,1)S(1)}, bf16[2,80,320]{2,1,0:T(8,128)(2,1)S(1)}, u32[]{:S(2)}, u32[]{:S(2)}) %collective-permute-start.27) | collective-permute-done | bytes 102432 | tf_op jit(solution)/shard_map/ppermute | solution.py:33
  132.5 5.0 %collective-permute-done.29 = bf16[80,320]{1,0:T(8,128)(2,1)S(1)} collective-permute-done((bf16[80,320]{1,0:T(8,128)(2,1)S(1)}, bf16[80,320]{1,0:T(8,128)(2,1)S(1)}, u32[]{:S(2)}, u32[]{:S(2)}) %collective-permute-start.29) | collective-permute-done | bytes 51232 | tf_op jit(solution)/shard_map/ppermute | solution.py:33
  140.2 4.9 %backward.2.refs_0_ = bf16[3,320,512]{2,1,0:T(8,128)(2,1)} custom-call(s32[1]{0:T(128)S(6)} %copy.14.count_ref, bf16[3,320,512]{2,1,0:T(8,128)(2,1)S(1)} %bitcast.33, bf16[320,512]{1,0:T(8,128)(2,1)S(1)} %get-tuple-element.23.refs_1_.refs_2_, bf16[320,512]{1,0:T(8,128)(2,1)S(1)} %collective-permute-done.17.refs_2_.refs_3_, ...), custom_call_target="tpu_custom_call" | custom-call | flops 603979776 | bytes 1572864 | tf_op jit(solution)/shard_map/backward/pallas_call | solution.py:139
  145.1 3.5 %backward.3 = bf16[3,320,512]{2,1,0:T(8,128)(2,1)} custom-call(s32[1]{0:T(128)S(6)} %copy.14.count_ref, bf16[3,320,512]{2,1,0:T(8,128)(2,1)} %backward.2.refs_0_, bf16[3,320,512]{2,1,0:T(8,128)(2,1)S(1)} %bitcast.34, bf16[320,512]{1,0:T(8,128)(2,1)S(1)} %get-tuple-element.23.refs_1_.refs_2_, ...), custom_call_target="tpu_custom_call", output_to_operand_aliasing={{}: (1, {})} | custom-call | flops 402653184 | bytes 1048576 | tf_op jit(solution)/shard_map/backward/pallas_call | solution.py:139
  (70 shorter events, 28.6 us)
Async XLA Ops:
  6.3 58.8 %collective-permute-start.9 = (bf16[320,512]{1,0:T(8,128)(2,1)S(1)}, bf16[320,512]{1,0:T(8,128)(2,1)S(1)}, u32[]{:S(2)}, u32[]{:S(2)}) collective-permute-start(bf16[320,512]{1,0:T(8,128)(2,1)S(1)} %forward.1.refs_0_), channel_id=1, source_target_pairs={{0,6},{1,7},{2,0},{3,1},{4,2},{5,3},{6,4},{7,5},{8,14},{9,15},{10,... | collective-permute-start | bytes 983048 | tf_op jit(solution)/shard_map/ppermute | solution.py:40
  9.7 54.0 %collective-permute-start.11 = (bf16[320,512]{1,0:T(8,128)(2,1)S(1)}, bf16[320,512]{1,0:T(8,128)(2,1)S(1)}, u32[]{:S(2)}, u32[]{:S(2)}) collective-permute-start(bf16[320,512]{1,0:T(8,128)(2,1)S(1)} %forward.1.refs_0_), channel_id=1, source_target_pairs={{0,4},{1,5},{2,6},{3,7},{4,0},{5,1},{6,2},{7,3},{8,12},{9,13},{10,... | collective-permute-start | bytes 983048 | tf_op jit(solution)/shard_map/ppermute | solution.py:40
  10.2 50.8 %collective-permute-start.12 = (bf16[320,512]{1,0:T(8,128)(2,1)S(1)}, bf16[320,512]{1,0:T(8,128)(2,1)S(1)}, u32[]{:S(2)}, u32[]{:S(2)}) collective-permute-start(bf16[320,512]{1,0:T(8,128)(2,1)S(1)} %forward.1.refs_0_), channel_id=1, source_target_pairs={{0,1},{1,0},{2,3},{3,2},{4,5},{5,4},{6,7},{7,6},{8,9},{9,8},{10,11... | collective-permute-start | bytes 983048 | tf_op jit(solution)/shard_map/ppermute | solution.py:40
  13.1 11.1 %collective-permute-start.1 = (bf16[80,320]{1,0:T(8,128)(2,1)S(1)}, bf16[80,320]{1,0:T(8,128)(2,1)S(1)}, u32[]{:S(2)}, u32[]{:S(2)}) collective-permute-start(bf16[80,320]{1,0:T(8,128)(2,1)S(1)} %bitcast.42), channel_id=1, source_target_pairs={{0,128},{2,96},{6,160},{4,64},{1,192},{3,32},{7,224},{5,0},{8,136}... | collective-permute-start | bytes 153608 | tf_op jit(solution)/shard_map/ppermute | solution.py:55
  20.1 43.6 %collective-permute-start = (bf16[320,512]{1,0:T(8,128)(2,1)S(1)}, bf16[320,512]{1,0:T(8,128)(2,1)S(1)}, u32[]{:S(2)}, u32[]{:S(2)}) collective-permute-start(bf16[320,512]{1,0:T(8,128)(2,1)S(1)} %slice_bitcast_fusion), channel_id=1, source_target_pairs={{0,128},{8,136},{16,144},{24,152},{32,160},{40,168},{48,176},{56,1... | collective-permute-start | bytes 983048 | tf_op jit(solution)/shard_map/ppermute | solution.py:33
  24.2 17.1 %collective-permute-start.2 = (bf16[80,320]{1,0:T(8,128)(2,1)S(1)}, bf16[80,320]{1,0:T(8,128)(2,1)S(1)}, u32[]{:S(2)}, u32[]{:S(2)}) collective-permute-start(bf16[80,320]{1,0:T(8,128)(2,1)S(1)} %collective-permute-done.1), channel_id=1, source_target_pairs={{0,128},{8,136},{16,144},{24,152},{32,160},{40,168},{48,176},{56,1... | collective-permute-start | bytes 153608 | tf_op jit(solution)/shard_map/ppermute | solution.py:33
  45.1 10.2 %collective-permute-start.4 = (bf16[2,80,320]{2,1,0:T(8,128)(2,1)S(1)}, bf16[2,80,320]{2,1,0:T(8,128)(2,1)S(1)}, u32[]{:S(2)}, u32[]{:S(2)}) collective-permute-start(bf16[2,80,320]{2,1,0:T(8,128)(2,1)S(1)} %pad_maximum_fusion), channel_id=1, source_target_pairs={{0,64},{8,72},{16,80},{24,88},{32,96},{40,104},{48,112},{56,120},{... | collective-permute-start | bytes 307208 | tf_op jit(solution)/shard_map/ppermute | solution.py:33
  63.7 8.0 %collective-permute-start.14 = (bf16[320,512]{1,0:T(8,128)(2,1)S(1)}, bf16[320,512]{1,0:T(8,128)(2,1)S(1)}, u32[]{:S(2)}, u32[]{:S(2)}) collective-permute-start(bf16[320,512]{1,0:T(8,128)(2,1)S(1)} %collective-permute-done.12.refs_4_), channel_id=1, source_target_pairs={{0,2},{1,3},{2,4},{3,5},{4,6},{5,7},{6,0},{7,1},{8,10},{9,11},{10,... | collective-permute-start | bytes 983048 | tf_op jit(solution)/shard_map/ppermute | solution.py:40
  63.7 8.0 %collective-permute-start.15 = (bf16[320,512]{1,0:T(8,128)(2,1)S(1)}, bf16[320,512]{1,0:T(8,128)(2,1)S(1)}, u32[]{:S(2)}, u32[]{:S(2)}) collective-permute-start(bf16[320,512]{1,0:T(8,128)(2,1)S(1)} %collective-permute-done.11.refs_3_), channel_id=1, source_target_pairs={{0,1},{1,0},{2,3},{3,2},{4,5},{5,4},{6,7},{7,6},{8,9},{9,8},{10,11... | collective-permute-start | bytes 983048 | tf_op jit(solution)/shard_map/ppermute | solution.py:40
  65.2 20.1 %collective-permute-start.6 = (bf16[8,80,320]{2,1,0:T(8,128)(2,1)S(1)}, bf16[8,80,320]{2,1,0:T(8,128)(2,1)S(1)}, u32[]{:S(2)}, u32[]{:S(2)}) collective-permute-start(bf16[8,80,320]{2,1,0:T(8,128)(2,1)S(1)} %constant_dynamic-update-slice_fusion.w0_ref), channel_id=1, source_target_pairs={{0,16},{8,24},{16,0},{24,8},{32,48},{40,56},{48,32},{56,40},{64,80... | collective-permute-start | bytes 1228808 | tf_op jit(solution)/shard_map/ppermute | solution.py:33
  73.4 19.8 %collective-permute-start.24 = (bf16[2,8,80,320]{3,2,1,0:T(8,128)(2,1)S(1)}, bf16[2,8,80,320]{3,2,1,0:T(8,128)(2,1)S(1)}, u32[]{:S(2)}, u32[]{:S(2)}) collective-permute-start(bf16[2,8,80,320]{3,2,1,0:T(8,128)(2,1)S(1)} %get-tuple-element.32), channel_id=1, source_target_pairs={{0,8},{8,0},{16,24},{24,16},{32,40},{40,32},{48,56},{56,48},{64,72... | collective-permute-start | bytes 2457608 | tf_op jit(solution)/shard_map/ppermute | solution.py:33
  90.3 11.1 %collective-permute-start.22 = (bf16[320,512]{1,0:T(8,128)(2,1)S(1)}, bf16[320,512]{1,0:T(8,128)(2,1)S(1)}, u32[]{:S(2)}, u32[]{:S(2)}) collective-permute-start(bf16[320,512]{1,0:T(8,128)(2,1)S(1)} %get-tuple-element.30), channel_id=1, source_target_pairs={{0,6},{1,7},{2,0},{3,1},{4,2},{5,3},{6,4},{7,5},{8,14},{9,15},{10,... | collective-permute-start | bytes 983048 | tf_op jit(solution)/shard_map/ppermute | solution.py:40
  93.2 10.1 %collective-permute-start.21 = (bf16[320,512]{1,0:T(8,128)(2,1)S(1)}, bf16[320,512]{1,0:T(8,128)(2,1)S(1)}, u32[]{:S(2)}, u32[]{:S(2)}) collective-permute-start(bf16[320,512]{1,0:T(8,128)(2,1)S(1)} %get-tuple-element.29), channel_id=1, source_target_pairs={{0,2},{1,3},{2,4},{3,5},{4,6},{5,7},{6,0},{7,1},{8,10},{9,11},{10,... | collective-permute-start | bytes 983048 | tf_op jit(solution)/shard_map/ppermute | solution.py:40
  93.3 12.2 %collective-permute-start.25 = (bf16[8,80,320]{2,1,0:T(8,128)(2,1)S(1)}, bf16[8,80,320]{2,1,0:T(8,128)(2,1)S(1)}, u32[]{:S(2)}, u32[]{:S(2)}) collective-permute-start(bf16[8,80,320]{2,1,0:T(8,128)(2,1)S(1)} %fusion.1), channel_id=1, source_target_pairs={{0,16},{8,24},{16,0},{24,8},{32,48},{40,56},{48,32},{56,40},{64,80... | collective-permute-start | bytes 1228808 | tf_op jit(solution)/shard_map/ppermute | solution.py:33
  96.1 34.4 %collective-permute-start.16 = (bf16[320,512]{1,0:T(8,128)(2,1)S(1)}, bf16[320,512]{1,0:T(8,128)(2,1)S(1)}, u32[]{:S(2)}, u32[]{:S(2)}) collective-permute-start(bf16[320,512]{1,0:T(8,128)(2,1)S(1)} %get-tuple-element.22), channel_id=1, source_target_pairs={{0,128},{8,136},{16,144},{24,152},{32,160},{40,168},{48,176},{56,1... | collective-permute-start | bytes 983048 | tf_op jit(solution)/shard_map/ppermute | solution.py:33
  101.4 38.8 %collective-permute-start.17 = (bf16[320,512]{1,0:T(8,128)(2,1)S(1)}, bf16[320,512]{1,0:T(8,128)(2,1)S(1)}, u32[]{:S(2)}, u32[]{:S(2)}) collective-permute-start(bf16[320,512]{1,0:T(8,128)(2,1)S(1)} %get-tuple-element.24), channel_id=1, source_target_pairs={{0,2},{1,3},{2,4},{3,5},{4,6},{5,7},{6,0},{7,1},{8,10},{9,11},{10,... | collective-permute-start | bytes 983048 | tf_op jit(solution)/shard_map/ppermute | solution.py:40
  101.4 13.1 %collective-permute-start.19 = (bf16[320,512]{1,0:T(8,128)(2,1)S(1)}, bf16[320,512]{1,0:T(8,128)(2,1)S(1)}, u32[]{:S(2)}, u32[]{:S(2)}) collective-permute-start(bf16[320,512]{1,0:T(8,128)(2,1)S(1)} %get-tuple-element.27), channel_id=1, source_target_pairs={{0,1},{1,0},{2,3},{3,2},{4,5},{5,4},{6,7},{7,6},{8,9},{9,8},{10,11... | collective-permute-start | bytes 983048 | tf_op jit(solution)/shard_map/ppermute | solution.py:40
  105.8 12.2 %collective-permute-start.28 = (bf16[2,80,320]{2,1,0:T(8,128)(2,1)S(1)}, bf16[2,80,320]{2,1,0:T(8,128)(2,1)S(1)}, u32[]{:S(2)}, u32[]{:S(2)}) collective-permute-start(bf16[2,80,320]{2,1,0:T(8,128)(2,1)S(1)} %get-tuple-element.34), channel_id=1, source_target_pairs={{0,96},{8,104},{16,112},{24,120},{32,64},{40,72},{48,80},{56,88},{... | collective-permute-start | bytes 307208 | tf_op jit(solution)/shard_map/ppermute | solution.py:33
  106.9 20.3 %collective-permute-start.27 = (bf16[2,80,320]{2,1,0:T(8,128)(2,1)S(1)}, bf16[2,80,320]{2,1,0:T(8,128)(2,1)S(1)}, u32[]{:S(2)}, u32[]{:S(2)}) collective-permute-start(bf16[2,80,320]{2,1,0:T(8,128)(2,1)S(1)} %get-tuple-element.35), channel_id=1, source_target_pairs={{0,64},{8,72},{16,80},{24,88},{32,96},{40,104},{48,112},{56,120},{... | collective-permute-start | bytes 307208 | tf_op jit(solution)/shard_map/ppermute | solution.py:33
  114.4 14.0 %collective-permute-start.26 = (bf16[2,80,320]{2,1,0:T(8,128)(2,1)S(1)}, bf16[2,80,320]{2,1,0:T(8,128)(2,1)S(1)}, u32[]{:S(2)}, u32[]{:S(2)}) collective-permute-start(bf16[2,80,320]{2,1,0:T(8,128)(2,1)S(1)} %get-tuple-element.33), channel_id=1, source_target_pairs={{0,32},{8,40},{16,48},{24,56},{32,0},{40,8},{48,16},{56,24},{64,96... | collective-permute-start | bytes 307208 | tf_op jit(solution)/shard_map/ppermute | solution.py:33
  118.0 22.2 %collective-permute-start.18 = (bf16[320,512]{1,0:T(8,128)(2,1)S(1)}, bf16[320,512]{1,0:T(8,128)(2,1)S(1)}, u32[]{:S(2)}, u32[]{:S(2)}) collective-permute-start(bf16[320,512]{1,0:T(8,128)(2,1)S(1)} %get-tuple-element.25), channel_id=1, source_target_pairs={{0,6},{1,7},{2,0},{3,1},{4,2},{5,3},{6,4},{7,5},{8,14},{9,15},{10,... | collective-permute-start | bytes 983048 | tf_op jit(solution)/shard_map/ppermute | solution.py:40
  127.2 13.0 %collective-permute-start.20 = (bf16[320,512]{1,0:T(8,128)(2,1)S(1)}, bf16[320,512]{1,0:T(8,128)(2,1)S(1)}, u32[]{:S(2)}, u32[]{:S(2)}) collective-permute-start(bf16[320,512]{1,0:T(8,128)(2,1)S(1)} %add_convert_fusion.2), channel_id=1, source_target_pairs={{0,4},{1,5},{2,6},{3,7},{4,0},{5,1},{6,2},{7,3},{8,12},{9,13},{10,... | collective-permute-start | bytes 983048 | tf_op jit(solution)/shard_map/ppermute | solution.py:40
  128.5 11.7 %collective-permute-start.23 = (bf16[320,512]{1,0:T(8,128)(2,1)S(1)}, bf16[320,512]{1,0:T(8,128)(2,1)S(1)}, u32[]{:S(2)}, u32[]{:S(2)}) collective-permute-start(bf16[320,512]{1,0:T(8,128)(2,1)S(1)} %add_convert_fusion.1), channel_id=1, source_target_pairs={{0,1},{1,0},{2,3},{3,2},{4,5},{5,4},{6,7},{7,6},{8,9},{9,8},{10,11... | collective-permute-start | bytes 983048 | tf_op jit(solution)/shard_map/ppermute | solution.py:40
  137.6 11.1 %collective-permute-start.30 = (bf16[80,320]{1,0:T(8,128)(2,1)S(1)}, bf16[80,320]{1,0:T(8,128)(2,1)S(1)}, u32[]{:S(2)}, u32[]{:S(2)}) collective-permute-start(bf16[80,320]{1,0:T(8,128)(2,1)S(1)} %fusion.2), channel_id=1, source_target_pairs={{128,0},{96,2},{160,6},{64,4},{192,1},{32,3},{224,7},{0,5},{136,8}... | collective-permute-start | bytes 153608 | tf_op jit(solution)/shard_map/ppermute | solution.py:55
  (11 other events, 100.9 us)

commit v4 on v3

--- a/solution.py
+++ b/solution.py
@@ -91,8 +91,8 @@
     ctx_ref[...] = jnp.where(live, context, 0.0).astype(BF16)
 
 
-def backward_kernel(skipped, count_ref, *refs):
-    qkv_ref, grad_refs, out_ref = refs[skipped], refs[skipped + 1 : -1], refs[-1]
+def backward_kernel(count_ref, qkv_ref, *refs):
+    grad_refs, out_ref = refs[:-1], refs[-1]
     count = count_ref[0]
     grad = functools.reduce(lambda a, b: a + b, [r[...].astype(F32) for r in grad_refs])
     live = lax.broadcasted_iota(jnp.int32, (1, grad.shape[1]), 1) < count
@@ -131,25 +131,21 @@
     )(count, qkv)
 
 
-def backward(count, qkv, grads, first, heads, earlier=None):
-    length = qkv.shape[2]
-    plane = pl.BlockSpec((HEAD_DIM, length), lambda h: (h + first, 0))
-    planes = pl.BlockSpec((3, HEAD_DIM, length), lambda h: (0, h + first, 0))
-    before = [] if earlier is None else [earlier]
-    return pl.pallas_call(
-        functools.partial(backward_kernel, len(before)),
+def backward(count, qkv, grads):
+    _, columns, length = qkv.shape
+    heads = columns // HEAD_DIM
+    plane = pl.BlockSpec((HEAD_DIM, length), lambda h: (h, 0))
+    planes = pl.BlockSpec((3, HEAD_DIM, length), lambda h: (0, h, 0))
+    return pl.pallas_call(
+        backward_kernel,
         name="backward",
         grid=(heads,),
-        in_specs=[SMEM]
-        + [pl.BlockSpec(memory_space=pl.ANY)] * len(before)
-        + [planes]
-        + [plane] * len(grads),
+        in_specs=[SMEM, planes] + [plane] * len(grads),
         out_specs=planes,
         out_shape=jax.ShapeDtypeStruct(qkv.shape, BF16),
-        input_output_aliases={1: 0} if before else {},
         compiler_params=pltpu.CompilerParams(vmem_limit_bytes=16 << 20),
         cost_estimate=kernel_cost(6, heads, length),
-    )(count, *before, qkv, *grads)
+    )(count, qkv, *grads)
 
 
 def grad_partial_kernel(cot_ref, w0_ref, wy_ref, wc_ref, wcy_ref, all_ref, *out_refs):
@@ -260,7 +256,7 @@
     block[1, 0] = along_tensor(ctx, -1, 0)
     block[-1, 1] = along_tensor(block[0, 1], 1, 0)
     block[1, 1] = along_tensor(block[0, 1], -1, 0)
-    block[2, 1] = along_tensor(block[2, 0], 0, 1)
+    block[2, 1] = along_tensor(block[0, 1], 2, 0)
     blocks = [block[place] for place in PLACES]
 
     two = jnp.stack([moved, exchanged(moved, 16)])
@@ -273,12 +269,17 @@
     weight, *parts = grad_partial(cot, w0, wy, wc, wcy)
     part = dict(zip(PLACES, parts))
 
-    from_other = along_tensor(part[2, 1], 0, 1)
-    from_left = along_tensor(part[1, 1], 1, 0)
-    from_right = along_tensor(part[-1, 1], -1, 0)
-    got = [along_tensor(part[1, 0], 1, 0), along_tensor(part[-1, 0], -1, 0)]
-    got.append(along_tensor(added(part[2, 0], from_other), 2, 0))
-    got.append(along_tensor(added(part[0, 1], from_left, from_right), 0, 1))
+    across = [
+        along_tensor(part[2, 1], 2, 0),
+        along_tensor(part[1, 1], 1, 0),
+        along_tensor(part[-1, 1], -1, 0),
+    ]
+    got = [
+        along_tensor(part[2, 0], 2, 0),
+        along_tensor(part[1, 0], 1, 0),
+        along_tensor(part[-1, 0], -1, 0),
+        along_tensor(added(part[0, 1], *across), 0, 1),
+    ]
 
     keep, send = weight_partial(cot, blocks)
     both = exchanged(send, 1)
@@ -294,10 +295,7 @@
     layer_out = jnp.transpose(jnp.stack([home, returned]), (0, 2, 1))
 
     grads = (part[0, 0], *got)
-    heads = qkv.shape[1] // HEAD_DIM
-    early = heads - heads // 2
-    grad_qkv = backward(residue_counts, qkv, grads, 0, early)
-    grad_qkv = backward(residue_counts, qkv, grads, early, heads - early, grad_qkv)
+    grad_qkv = backward(residue_counts, qkv, grads)
     return layer_out, jnp.transpose(grad_qkv, (0, 2, 1)), grad_weight
 
 

time: 150 us -> 146 us (0.973)
  waiting for transfers between devices: 58.7 us -> 52.8 us
  starting transfers between devices: 67.7 us -> 70.3 us
    ppermute x15, waiting for transfers between devices: 44.9 us -> 21.6 us  [along_dp(): return lax.ppermute(value, 'dp', [(i, to(i)) for i in range(N_DP)])]
    ppermute x14, waiting for transfers between devices: 13.7 us -> 27.6 us  [along_tensor(): return lax.ppermute(value, 'tensor', [(i, to(i)) for i in range(N_TENSOR)])]
    ppermute x14, starting transfers between devices: 19.7 us -> 31 us  [along_tensor(): return lax.ppermute(value, 'tensor', [(i, to(i)) for i in range(N_TENSOR)])]
    ppermute x2, starting transfers between devices: 9.52 us -> 1.04 us  [swapped(): return lax.ppermute(value, ('dp', 'tensor'), pairs)]
    ppermute x2, waiting for transfers between devices: 0.01 us -> 3.6 us  [swapped(): return lax.ppermute(value, ('dp', 'tensor'), pairs)]
    pallas_call x2 -> x1, Pallas kernels: 8.43 us -> 7.76 us  [backward(): pl.pallas_call(backward_kernel, name='backward', grid=(heads,), in_specs=...]
  transfers between devices with their start and end apart: 31 -> 31, of which waited for: 13 -> 12; matrix products, arithmetic and copies ran while one was open for 1% -> 1% of each run, Pallas kernels for 9% -> 9%
where the time goes in v4:
time: 146 us; the launch traced here: 145 us
  starting transfers between devices  70.3 us (48%)
  waiting for transfers between devices  52.8 us (36%)
  Pallas kernels  16.5 us (11%)
  other arithmetic  2.17 us (1%)
  between operations  2.15 us (1%)
    ppermute x15, starting transfers between devices, along_dp(): return lax.ppermute(value, 'dp', [(i, to(i)) for i in range(N_DP)])  38.3 us
    ppermute x14, starting transfers between devices, along_tensor(): return lax.ppermute(value, 'tensor', [(i, to(i)) for i in range(N_TENSOR)])  31 us
    ppermute x14, waiting for transfers between devices, along_tensor(): return lax.ppermute(value, 'tensor', [(i, to(i)) for i in range(N_TENSOR)])  27.6 us
    ppermute x15, waiting for transfers between devices, along_dp(): return lax.ppermute(value, 'dp', [(i, to(i)) for i in range(N_DP)])  21.6 us
    pallas_call x1, Pallas kernels, backward(): pl.pallas_call(backward_kernel, name='backward', grid=(heads,), in_specs=...  7.76 us
    pallas_call x1, Pallas kernels, forward(): pl.pallas_call(forward_kernel, name='forward', grid=(heads,), in_specs=[S...  3.82 us
    ppermute x2, waiting for transfers between devices, swapped(): return lax.ppermute(value, ('dp', 'tensor'), pairs)  3.6 us
  transfers between devices with their start and end apart: 31, of which 12 were waited for; matrix products, arithmetic and copies ran while one was open for 1% of the time, Pallas kernels for 9%

profile of v4, /device:TPU:1, one launch (start us, length us, event | category | flops | bytes accessed | tf_op | source)
XLA Modules:
  0.0 145.3 jit_solution(17227703069115969686)
XLA Ops:
  2.5 3.8 %forward.1.refs_0_ = bf16[320,512]{1,0:T(8,128)(2,1)S(1)} custom-call(s32[1]{0:T(128)S(6)} %copy.12.count_ref, bf16[3,320,512]{2,1,0:T(8,128)(2,1)S(1)} %bitcast.33), custom_call_target="tpu_custom_call" | custom-call | flops 335544320 | bytes 2621440 | tf_op jit(solution)/shard_map/forward/pallas_call | solution.py:122
  6.3 3.8 %collective-permute-start.12 = (bf16[320,512]{1,0:T(8,128)(2,1)S(1)}, bf16[320,512]{1,0:T(8,128)(2,1)S(1)}, u32[]{:S(2)}, u32[]{:S(2)}) collective-permute-start(bf16[320,512]{1,0:T(8,128)(2,1)S(1)} %forward.1.refs_0_), channel_id=1, source_target_pairs={{0,1},{1,0},{2,3},{3,2},{4,5},{5,4},{6,7},{7,6},{8,9},{9,8},{10,11... | collective-permute-start | bytes 983048 | tf_op jit(solution)/shard_map/ppermute | solution.py:40
  10.2 7.0 %collective-permute-start = (bf16[320,512]{1,0:T(8,128)(2,1)S(1)}, bf16[320,512]{1,0:T(8,128)(2,1)S(1)}, u32[]{:S(2)}, u32[]{:S(2)}) collective-permute-start(bf16[320,512]{1,0:T(8,128)(2,1)S(1)} %slice_bitcast_fusion), channel_id=1, source_target_pairs={{0,128},{8,136},{16,144},{24,152},{32,160},{40,168},{48,176},{56,1... | collective-permute-start | bytes 983048 | tf_op jit(solution)/shard_map/ppermute | solution.py:33
  17.2 2.5 %collective-permute-start.9 = (bf16[320,512]{1,0:T(8,128)(2,1)S(1)}, bf16[320,512]{1,0:T(8,128)(2,1)S(1)}, u32[]{:S(2)}, u32[]{:S(2)}) collective-permute-start(bf16[320,512]{1,0:T(8,128)(2,1)S(1)} %forward.1.refs_0_), channel_id=1, source_target_pairs={{0,6},{1,7},{2,0},{3,1},{4,2},{5,3},{6,4},{7,5},{8,14},{9,15},{10,... | collective-permute-start | bytes 983048 | tf_op jit(solution)/shard_map/ppermute | solution.py:40
  19.7 2.7 %collective-permute-start.10 = (bf16[320,512]{1,0:T(8,128)(2,1)S(1)}, bf16[320,512]{1,0:T(8,128)(2,1)S(1)}, u32[]{:S(2)}, u32[]{:S(2)}) collective-permute-start(bf16[320,512]{1,0:T(8,128)(2,1)S(1)} %forward.1.refs_0_), channel_id=1, source_target_pairs={{0,2},{1,3},{2,4},{3,5},{4,6},{5,7},{6,0},{7,1},{8,10},{9,11},{10,... | collective-permute-start | bytes 983048 | tf_op jit(solution)/shard_map/ppermute | solution.py:40
  23.1 3.6 %collective-permute-done.1 = bf16[80,320]{1,0:T(8,128)(2,1)S(1)} collective-permute-done((bf16[80,320]{1,0:T(8,128)(2,1)S(1)}, bf16[80,320]{1,0:T(8,128)(2,1)S(1)}, u32[]{:S(2)}, u32[]{:S(2)}) %collective-permute-start.1) | collective-permute-done | bytes 51232 | tf_op jit(solution)/shard_map/ppermute | solution.py:55
  26.7 5.6 %collective-permute-start.2 = (bf16[80,320]{1,0:T(8,128)(2,1)S(1)}, bf16[80,320]{1,0:T(8,128)(2,1)S(1)}, u32[]{:S(2)}, u32[]{:S(2)}) collective-permute-start(bf16[80,320]{1,0:T(8,128)(2,1)S(1)} %collective-permute-done.1), channel_id=1, source_target_pairs={{0,128},{8,136},{16,144},{24,152},{32,160},{40,168},{48,176},{56,1... | collective-permute-start | bytes 153608 | tf_op jit(solution)/shard_map/ppermute | solution.py:33
  32.4 4.6 %collective-permute-done.2 = bf16[80,320]{1,0:T(8,128)(2,1)S(1)} collective-permute-done((bf16[80,320]{1,0:T(8,128)(2,1)S(1)}, bf16[80,320]{1,0:T(8,128)(2,1)S(1)}, u32[]{:S(2)}, u32[]{:S(2)}) %collective-permute-start.2) | collective-permute-done | bytes 51232 | tf_op jit(solution)/shard_map/ppermute | solution.py:33
  37.0 5.3 %collective-permute-start.11 = (bf16[320,512]{1,0:T(8,128)(2,1)S(1)}, bf16[320,512]{1,0:T(8,128)(2,1)S(1)}, u32[]{:S(2)}, u32[]{:S(2)}) collective-permute-start(bf16[320,512]{1,0:T(8,128)(2,1)S(1)} %forward.1.refs_0_), channel_id=1, source_target_pairs={{0,4},{1,5},{2,6},{3,7},{4,0},{5,1},{6,2},{7,3},{8,12},{9,13},{10,... | collective-permute-start | bytes 983048 | tf_op jit(solution)/shard_map/ppermute | solution.py:40
  42.3 2.3 %collective-permute-start.13 = (bf16[320,512]{1,0:T(8,128)(2,1)S(1)}, bf16[320,512]{1,0:T(8,128)(2,1)S(1)}, u32[]{:S(2)}, u32[]{:S(2)}) collective-permute-start(bf16[320,512]{1,0:T(8,128)(2,1)S(1)} %collective-permute-done.12.refs_4_), channel_id=1, source_target_pairs={{0,6},{1,7},{2,0},{3,1},{4,2},{5,3},{6,4},{7,5},{8,14},{9,15},{10,... | collective-permute-start | bytes 983048 | tf_op jit(solution)/shard_map/ppermute | solution.py:40
  46.0 2.8 %collective-permute-start.3 = (bf16[2,80,320]{2,1,0:T(8,128)(2,1)S(1)}, bf16[2,80,320]{2,1,0:T(8,128)(2,1)S(1)}, u32[]{:S(2)}, u32[]{:S(2)}) collective-permute-start(bf16[2,80,320]{2,1,0:T(8,128)(2,1)S(1)} %pad_maximum_fusion), channel_id=1, source_target_pairs={{0,32},{8,40},{16,48},{24,56},{32,0},{40,8},{48,16},{56,24},{64,96... | collective-permute-start | bytes 307208 | tf_op jit(solution)/shard_map/ppermute | solution.py:33
  48.8 2.7 %collective-permute-start.4 = (bf16[2,80,320]{2,1,0:T(8,128)(2,1)S(1)}, bf16[2,80,320]{2,1,0:T(8,128)(2,1)S(1)}, u32[]{:S(2)}, u32[]{:S(2)}) collective-permute-start(bf16[2,80,320]{2,1,0:T(8,128)(2,1)S(1)} %pad_maximum_fusion), channel_id=1, source_target_pairs={{0,64},{8,72},{16,80},{24,88},{32,96},{40,104},{48,112},{56,120},{... | collective-permute-start | bytes 307208 | tf_op jit(solution)/shard_map/ppermute | solution.py:33
  51.5 9.0 %collective-permute-done.13.refs_5_ = bf16[320,512]{1,0:T(8,128)(2,1)S(1)} collective-permute-done((bf16[320,512]{1,0:T(8,128)(2,1)S(1)}, bf16[320,512]{1,0:T(8,128)(2,1)S(1)}, u32[]{:S(2)}, u32[]{:S(2)}) %collective-permute-start.13) | collective-permute-done | bytes 327712 | tf_op jit(solution)/shard_map/ppermute | solution.py:40
  64.6 3.5 %collective-permute-start.24 = (bf16[2,8,80,320]{3,2,1,0:T(8,128)(2,1)S(1)}, bf16[2,8,80,320]{3,2,1,0:T(8,128)(2,1)S(1)}, u32[]{:S(2)}, u32[]{:S(2)}) collective-permute-start(bf16[2,8,80,320]{3,2,1,0:T(8,128)(2,1)S(1)} %get-tuple-element.32), channel_id=1, source_target_pairs={{0,8},{8,0},{16,24},{24,16},{32,40},{40,32},{48,56},{56,48},{64,72... | collective-permute-start | bytes 2457608 | tf_op jit(solution)/shard_map/ppermute | solution.py:33
  70.1 9.9 %collective-permute-done.6.wy_ref = bf16[8,80,320]{2,1,0:T(8,128)(2,1)S(1)} collective-permute-done((bf16[8,80,320]{2,1,0:T(8,128)(2,1)S(1)}, bf16[8,80,320]{2,1,0:T(8,128)(2,1)S(1)}, u32[]{:S(2)}, u32[]{:S(2)}) %collective-permute-start.6) | collective-permute-done | bytes 409632 | tf_op jit(solution)/shard_map/ppermute | solution.py:33
  86.7 4.8 %collective-permute-start.16 = (bf16[320,512]{1,0:T(8,128)(2,1)S(1)}, bf16[320,512]{1,0:T(8,128)(2,1)S(1)}, u32[]{:S(2)}, u32[]{:S(2)}) collective-permute-start(bf16[320,512]{1,0:T(8,128)(2,1)S(1)} %get-tuple-element.22), channel_id=1, source_target_pairs={{0,128},{8,136},{16,144},{24,152},{32,160},{40,168},{48,176},{56,1... | collective-permute-start | bytes 983048 | tf_op jit(solution)/shard_map/ppermute | solution.py:33
  91.8 3.6 %collective-permute-start.22 = (bf16[320,512]{1,0:T(8,128)(2,1)S(1)}, bf16[320,512]{1,0:T(8,128)(2,1)S(1)}, u32[]{:S(2)}, u32[]{:S(2)}) collective-permute-start(bf16[320,512]{1,0:T(8,128)(2,1)S(1)} %get-tuple-element.30), channel_id=1, source_target_pairs={{0,6},{1,7},{2,0},{3,1},{4,2},{5,3},{6,4},{7,5},{8,14},{9,15},{10,... | collective-permute-start | bytes 983048 | tf_op jit(solution)/shard_map/ppermute | solution.py:40
  97.0 10.5 %collective-permute-done.22 = bf16[320,512]{1,0:T(8,128)(2,1)S(1)} collective-permute-done((bf16[320,512]{1,0:T(8,128)(2,1)S(1)}, bf16[320,512]{1,0:T(8,128)(2,1)S(1)}, u32[]{:S(2)}, u32[]{:S(2)}) %collective-permute-start.22) | collective-permute-done | bytes 327712 | tf_op jit(solution)/shard_map/ppermute | solution.py:40
  111.8 3.9 %collective-permute-done.20 = bf16[320,512]{1,0:T(8,128)(2,1)S(1)} collective-permute-done((bf16[320,512]{1,0:T(8,128)(2,1)S(1)}, bf16[320,512]{1,0:T(8,128)(2,1)S(1)}, u32[]{:S(2)}, u32[]{:S(2)}) %collective-permute-start.20) | collective-permute-done | bytes 327712 | tf_op jit(solution)/shard_map/ppermute | solution.py:40
  115.7 3.7 %collective-permute-start.26 = (bf16[2,80,320]{2,1,0:T(8,128)(2,1)S(1)}, bf16[2,80,320]{2,1,0:T(8,128)(2,1)S(1)}, u32[]{:S(2)}, u32[]{:S(2)}) collective-permute-start(bf16[2,80,320]{2,1,0:T(8,128)(2,1)S(1)} %get-tuple-element.33), channel_id=1, source_target_pairs={{0,32},{8,40},{16,48},{24,56},{32,0},{40,8},{48,16},{56,24},{64,96... | collective-permute-start | bytes 307208 | tf_op jit(solution)/shard_map/ppermute | solution.py:33
  120.9 5.5 %collective-permute-start.19 = (bf16[320,512]{1,0:T(8,128)(2,1)S(1)}, bf16[320,512]{1,0:T(8,128)(2,1)S(1)}, u32[]{:S(2)}, u32[]{:S(2)}) collective-permute-start(bf16[320,512]{1,0:T(8,128)(2,1)S(1)} %get-tuple-element.26), channel_id=1, source_target_pairs={{0,6},{1,7},{2,0},{3,1},{4,2},{5,3},{6,4},{7,5},{8,14},{9,15},{10,... | collective-permute-start | bytes 983048 | tf_op jit(solution)/shard_map/ppermute | solution.py:40
  126.4 2.1 %collective-permute-start.23 = (bf16[320,512]{1,0:T(8,128)(2,1)S(1)}, bf16[320,512]{1,0:T(8,128)(2,1)S(1)}, u32[]{:S(2)}, u32[]{:S(2)}) collective-permute-start(bf16[320,512]{1,0:T(8,128)(2,1)S(1)} %add_convert_fusion.1), channel_id=1, source_target_pairs={{0,1},{1,0},{2,3},{3,2},{4,5},{5,4},{6,7},{7,6},{8,9},{9,8},{10,11... | collective-permute-start | bytes 983048 | tf_op jit(solution)/shard_map/ppermute | solution.py:40
  130.6 5.4 %collective-permute-done.29 = bf16[80,320]{1,0:T(8,128)(2,1)S(1)} collective-permute-done((bf16[80,320]{1,0:T(8,128)(2,1)S(1)}, bf16[80,320]{1,0:T(8,128)(2,1)S(1)}, u32[]{:S(2)}, u32[]{:S(2)}) %collective-permute-start.29) | collective-permute-done | bytes 51232 | tf_op jit(solution)/shard_map/ppermute | solution.py:33
  136.9 7.8 %backward.1 = bf16[3,320,512]{2,1,0:T(8,128)(2,1)} custom-call(s32[1]{0:T(128)S(6)} %copy.12.count_ref, bf16[3,320,512]{2,1,0:T(8,128)(2,1)S(1)} %bitcast.34, bf16[320,512]{1,0:T(8,128)(2,1)S(1)} %get-tuple-element.23.refs_0_, bf16[320,512]{1,0:T(8,128)(2,1)S(1)} %collective-permute-done.17.refs_1_, bf16[320,512]{1,0:T(8,128)(2,1)S(1)} %collective-permute-done.18.refs_2_, ...), custom_call_target="tpu_custom_call" | custom-call | flops 1006632960 | bytes 2621440 | tf_op jit(solution)/shard_map/backward/pallas_call | solution.py:139
  (68 shorter events, 26.6 us)
Async XLA Ops:
  6.3 36.0 %collective-permute-start.12 = (bf16[320,512]{1,0:T(8,128)(2,1)S(1)}, bf16[320,512]{1,0:T(8,128)(2,1)S(1)}, u32[]{:S(2)}, u32[]{:S(2)}) collective-permute-start(bf16[320,512]{1,0:T(8,128)(2,1)S(1)} %forward.1.refs_0_), channel_id=1, source_target_pairs={{0,1},{1,0},{2,3},{3,2},{4,5},{5,4},{6,7},{7,6},{8,9},{9,8},{10,11... | collective-permute-start | bytes 983048 | tf_op jit(solution)/shard_map/ppermute | solution.py:40
  10.2 34.5 %collective-permute-start = (bf16[320,512]{1,0:T(8,128)(2,1)S(1)}, bf16[320,512]{1,0:T(8,128)(2,1)S(1)}, u32[]{:S(2)}, u32[]{:S(2)}) collective-permute-start(bf16[320,512]{1,0:T(8,128)(2,1)S(1)} %slice_bitcast_fusion), channel_id=1, source_target_pairs={{0,128},{8,136},{16,144},{24,152},{32,160},{40,168},{48,176},{56,1... | collective-permute-start | bytes 983048 | tf_op jit(solution)/shard_map/ppermute | solution.py:33
  17.2 27.5 %collective-permute-start.9 = (bf16[320,512]{1,0:T(8,128)(2,1)S(1)}, bf16[320,512]{1,0:T(8,128)(2,1)S(1)}, u32[]{:S(2)}, u32[]{:S(2)}) collective-permute-start(bf16[320,512]{1,0:T(8,128)(2,1)S(1)} %forward.1.refs_0_), channel_id=1, source_target_pairs={{0,6},{1,7},{2,0},{3,1},{4,2},{5,3},{6,4},{7,5},{8,14},{9,15},{10,... | collective-permute-start | bytes 983048 | tf_op jit(solution)/shard_map/ppermute | solution.py:40
  19.7 26.3 %collective-permute-start.10 = (bf16[320,512]{1,0:T(8,128)(2,1)S(1)}, bf16[320,512]{1,0:T(8,128)(2,1)S(1)}, u32[]{:S(2)}, u32[]{:S(2)}) collective-permute-start(bf16[320,512]{1,0:T(8,128)(2,1)S(1)} %forward.1.refs_0_), channel_id=1, source_target_pairs={{0,2},{1,3},{2,4},{3,5},{4,6},{5,7},{6,0},{7,1},{8,10},{9,11},{10,... | collective-permute-start | bytes 983048 | tf_op jit(solution)/shard_map/ppermute | solution.py:40
  37.0 11.8 %collective-permute-start.11 = (bf16[320,512]{1,0:T(8,128)(2,1)S(1)}, bf16[320,512]{1,0:T(8,128)(2,1)S(1)}, u32[]{:S(2)}, u32[]{:S(2)}) collective-permute-start(bf16[320,512]{1,0:T(8,128)(2,1)S(1)} %forward.1.refs_0_), channel_id=1, source_target_pairs={{0,4},{1,5},{2,6},{3,7},{4,0},{5,1},{6,2},{7,3},{8,12},{9,13},{10,... | collective-permute-start | bytes 983048 | tf_op jit(solution)/shard_map/ppermute | solution.py:40
  42.3 18.2 %collective-permute-start.13 = (bf16[320,512]{1,0:T(8,128)(2,1)S(1)}, bf16[320,512]{1,0:T(8,128)(2,1)S(1)}, u32[]{:S(2)}, u32[]{:S(2)}) collective-permute-start(bf16[320,512]{1,0:T(8,128)(2,1)S(1)} %collective-permute-done.12.refs_4_), channel_id=1, source_target_pairs={{0,6},{1,7},{2,0},{3,1},{4,2},{5,3},{6,4},{7,5},{8,14},{9,15},{10,... | collective-permute-start | bytes 983048 | tf_op jit(solution)/shard_map/ppermute | solution.py:40
  44.7 16.2 %collective-permute-start.14 = (bf16[320,512]{1,0:T(8,128)(2,1)S(1)}, bf16[320,512]{1,0:T(8,128)(2,1)S(1)}, u32[]{:S(2)}, u32[]{:S(2)}) collective-permute-start(bf16[320,512]{1,0:T(8,128)(2,1)S(1)} %collective-permute-done.12.refs_4_), channel_id=1, source_target_pairs={{0,2},{1,3},{2,4},{3,5},{4,6},{5,7},{6,0},{7,1},{8,10},{9,11},{10,... | collective-permute-start | bytes 983048 | tf_op jit(solution)/shard_map/ppermute | solution.py:40
  44.7 18.1 %collective-permute-start.15 = (bf16[320,512]{1,0:T(8,128)(2,1)S(1)}, bf16[320,512]{1,0:T(8,128)(2,1)S(1)}, u32[]{:S(2)}, u32[]{:S(2)}) collective-permute-start(bf16[320,512]{1,0:T(8,128)(2,1)S(1)} %collective-permute-done.12.refs_4_), channel_id=1, source_target_pairs={{0,4},{1,5},{2,6},{3,7},{4,0},{5,1},{6,2},{7,3},{8,12},{9,13},{10,... | collective-permute-start | bytes 983048 | tf_op jit(solution)/shard_map/ppermute | solution.py:40
  46.0 22.1 %collective-permute-start.3 = (bf16[2,80,320]{2,1,0:T(8,128)(2,1)S(1)}, bf16[2,80,320]{2,1,0:T(8,128)(2,1)S(1)}, u32[]{:S(2)}, u32[]{:S(2)}) collective-permute-start(bf16[2,80,320]{2,1,0:T(8,128)(2,1)S(1)} %pad_maximum_fusion), channel_id=1, source_target_pairs={{0,32},{8,40},{16,48},{24,56},{32,0},{40,8},{48,16},{56,24},{64,96... | collective-permute-start | bytes 307208 | tf_op jit(solution)/shard_map/ppermute | solution.py:33
  48.8 19.4 %collective-permute-start.4 = (bf16[2,80,320]{2,1,0:T(8,128)(2,1)S(1)}, bf16[2,80,320]{2,1,0:T(8,128)(2,1)S(1)}, u32[]{:S(2)}, u32[]{:S(2)}) collective-permute-start(bf16[2,80,320]{2,1,0:T(8,128)(2,1)S(1)} %pad_maximum_fusion), channel_id=1, source_target_pairs={{0,64},{8,72},{16,80},{24,88},{32,96},{40,104},{48,112},{56,120},{... | collective-permute-start | bytes 307208 | tf_op jit(solution)/shard_map/ppermute | solution.py:33
  64.6 17.4 %collective-permute-start.24 = (bf16[2,8,80,320]{3,2,1,0:T(8,128)(2,1)S(1)}, bf16[2,8,80,320]{3,2,1,0:T(8,128)(2,1)S(1)}, u32[]{:S(2)}, u32[]{:S(2)}) collective-permute-start(bf16[2,8,80,320]{3,2,1,0:T(8,128)(2,1)S(1)} %get-tuple-element.32), channel_id=1, source_target_pairs={{0,8},{8,0},{16,24},{24,16},{32,40},{40,32},{48,56},{56,48},{64,72... | collective-permute-start | bytes 2457608 | tf_op jit(solution)/shard_map/ppermute | solution.py:33
  68.2 11.7 %collective-permute-start.6 = (bf16[8,80,320]{2,1,0:T(8,128)(2,1)S(1)}, bf16[8,80,320]{2,1,0:T(8,128)(2,1)S(1)}, u32[]{:S(2)}, u32[]{:S(2)}) collective-permute-start(bf16[8,80,320]{2,1,0:T(8,128)(2,1)S(1)} %constant_dynamic-update-slice_fusion.w0_ref), channel_id=1, source_target_pairs={{0,16},{8,24},{16,0},{24,8},{32,48},{40,56},{48,32},{56,40},{64,80... | collective-permute-start | bytes 1228808 | tf_op jit(solution)/shard_map/ppermute | solution.py:33
  69.1 13.9 %collective-permute-start.7 = (bf16[8,80,320]{2,1,0:T(8,128)(2,1)S(1)}, bf16[8,80,320]{2,1,0:T(8,128)(2,1)S(1)}, u32[]{:S(2)}, u32[]{:S(2)}) collective-permute-start(bf16[8,80,320]{2,1,0:T(8,128)(2,1)S(1)} %constant_dynamic-update-slice_fusion.w0_ref), channel_id=1, source_target_pairs={{0,8},{8,0},{16,24},{24,16},{32,40},{40,32},{48,56},{56,48},{64,72... | collective-permute-start | bytes 1228808 | tf_op jit(solution)/shard_map/ppermute | solution.py:33
  82.1 13.3 %collective-permute-start.25 = (bf16[8,80,320]{2,1,0:T(8,128)(2,1)S(1)}, bf16[8,80,320]{2,1,0:T(8,128)(2,1)S(1)}, u32[]{:S(2)}, u32[]{:S(2)}) collective-permute-start(bf16[8,80,320]{2,1,0:T(8,128)(2,1)S(1)} %fusion.1), channel_id=1, source_target_pairs={{0,16},{8,24},{16,0},{24,8},{32,48},{40,56},{48,32},{56,40},{64,80... | collective-permute-start | bytes 1228808 | tf_op jit(solution)/shard_map/ppermute | solution.py:33
  86.7 42.0 %collective-permute-start.16 = (bf16[320,512]{1,0:T(8,128)(2,1)S(1)}, bf16[320,512]{1,0:T(8,128)(2,1)S(1)}, u32[]{:S(2)}, u32[]{:S(2)}) collective-permute-start(bf16[320,512]{1,0:T(8,128)(2,1)S(1)} %get-tuple-element.22), channel_id=1, source_target_pairs={{0,128},{8,136},{16,144},{24,152},{32,160},{40,168},{48,176},{56,1... | collective-permute-start | bytes 983048 | tf_op jit(solution)/shard_map/ppermute | solution.py:33
  91.5 45.4 %collective-permute-start.17 = (bf16[320,512]{1,0:T(8,128)(2,1)S(1)}, bf16[320,512]{1,0:T(8,128)(2,1)S(1)}, u32[]{:S(2)}, u32[]{:S(2)}) collective-permute-start(bf16[320,512]{1,0:T(8,128)(2,1)S(1)} %get-tuple-element.24), channel_id=1, source_target_pairs={{0,4},{1,5},{2,6},{3,7},{4,0},{5,1},{6,2},{7,3},{8,12},{9,13},{10,... | collective-permute-start | bytes 983048 | tf_op jit(solution)/shard_map/ppermute | solution.py:40
  91.8 15.8 %collective-permute-start.22 = (bf16[320,512]{1,0:T(8,128)(2,1)S(1)}, bf16[320,512]{1,0:T(8,128)(2,1)S(1)}, u32[]{:S(2)}, u32[]{:S(2)}) collective-permute-start(bf16[320,512]{1,0:T(8,128)(2,1)S(1)} %get-tuple-element.30), channel_id=1, source_target_pairs={{0,6},{1,7},{2,0},{3,1},{4,2},{5,3},{6,4},{7,5},{8,14},{9,15},{10,... | collective-permute-start | bytes 983048 | tf_op jit(solution)/shard_map/ppermute | solution.py:40
  95.4 15.3 %collective-permute-start.21 = (bf16[320,512]{1,0:T(8,128)(2,1)S(1)}, bf16[320,512]{1,0:T(8,128)(2,1)S(1)}, u32[]{:S(2)}, u32[]{:S(2)}) collective-permute-start(bf16[320,512]{1,0:T(8,128)(2,1)S(1)} %get-tuple-element.29), channel_id=1, source_target_pairs={{0,2},{1,3},{2,4},{3,5},{4,6},{5,7},{6,0},{7,1},{8,10},{9,11},{10,... | collective-permute-start | bytes 983048 | tf_op jit(solution)/shard_map/ppermute | solution.py:40
  95.4 20.3 %collective-permute-start.20 = (bf16[320,512]{1,0:T(8,128)(2,1)S(1)}, bf16[320,512]{1,0:T(8,128)(2,1)S(1)}, u32[]{:S(2)}, u32[]{:S(2)}) collective-permute-start(bf16[320,512]{1,0:T(8,128)(2,1)S(1)} %get-tuple-element.28), channel_id=1, source_target_pairs={{0,4},{1,5},{2,6},{3,7},{4,0},{5,1},{6,2},{7,3},{8,12},{9,13},{10,... | collective-permute-start | bytes 983048 | tf_op jit(solution)/shard_map/ppermute | solution.py:40
  107.6 12.0 %collective-permute-start.28 = (bf16[2,80,320]{2,1,0:T(8,128)(2,1)S(1)}, bf16[2,80,320]{2,1,0:T(8,128)(2,1)S(1)}, u32[]{:S(2)}, u32[]{:S(2)}) collective-permute-start(bf16[2,80,320]{2,1,0:T(8,128)(2,1)S(1)} %get-tuple-element.34), channel_id=1, source_target_pairs={{0,96},{8,104},{16,112},{24,120},{32,64},{40,72},{48,80},{56,88},{... | collective-permute-start | bytes 307208 | tf_op jit(solution)/shard_map/ppermute | solution.py:33
  115.7 10.7 %collective-permute-start.26 = (bf16[2,80,320]{2,1,0:T(8,128)(2,1)S(1)}, bf16[2,80,320]{2,1,0:T(8,128)(2,1)S(1)}, u32[]{:S(2)}, u32[]{:S(2)}) collective-permute-start(bf16[2,80,320]{2,1,0:T(8,128)(2,1)S(1)} %get-tuple-element.33), channel_id=1, source_target_pairs={{0,32},{8,40},{16,48},{24,56},{32,0},{40,8},{48,16},{56,24},{64,96... | collective-permute-start | bytes 307208 | tf_op jit(solution)/shard_map/ppermute | solution.py:33
  119.6 17.3 %collective-permute-start.18 = (bf16[320,512]{1,0:T(8,128)(2,1)S(1)}, bf16[320,512]{1,0:T(8,128)(2,1)S(1)}, u32[]{:S(2)}, u32[]{:S(2)}) collective-permute-start(bf16[320,512]{1,0:T(8,128)(2,1)S(1)} %get-tuple-element.25), channel_id=1, source_target_pairs={{0,2},{1,3},{2,4},{3,5},{4,6},{5,7},{6,0},{7,1},{8,10},{9,11},{10,... | collective-permute-start | bytes 983048 | tf_op jit(solution)/shard_map/ppermute | solution.py:40
  120.9 16.0 %collective-permute-start.19 = (bf16[320,512]{1,0:T(8,128)(2,1)S(1)}, bf16[320,512]{1,0:T(8,128)(2,1)S(1)}, u32[]{:S(2)}, u32[]{:S(2)}) collective-permute-start(bf16[320,512]{1,0:T(8,128)(2,1)S(1)} %get-tuple-element.26), channel_id=1, source_target_pairs={{0,6},{1,7},{2,0},{3,1},{4,2},{5,3},{6,4},{7,5},{8,14},{9,15},{10,... | collective-permute-start | bytes 983048 | tf_op jit(solution)/shard_map/ppermute | solution.py:40
  126.4 10.5 %collective-permute-start.23 = (bf16[320,512]{1,0:T(8,128)(2,1)S(1)}, bf16[320,512]{1,0:T(8,128)(2,1)S(1)}, u32[]{:S(2)}, u32[]{:S(2)}) collective-permute-start(bf16[320,512]{1,0:T(8,128)(2,1)S(1)} %add_convert_fusion.1), channel_id=1, source_target_pairs={{0,1},{1,0},{2,3},{3,2},{4,5},{5,4},{6,7},{7,6},{8,9},{9,8},{10,11... | collective-permute-start | bytes 983048 | tf_op jit(solution)/shard_map/ppermute | solution.py:40
  (11 other events, 120.7 us)
